TPU v7x, 512 devices: a whole 4x8x8 slice. The times are simulated.
512 devices in a mesh: blk: 16 (over y_lo, x, core), seq: 32 (over z, y_hi).
Axes of the slice: x: 4, y: 8 (y_hi: 4, y_lo: 2; y = y_hi * 2 + y_lo), z: 8, core: 2. Of those that a mesh axis runs over, the one named last changes fastest.
Arguments:
- tokens: bfloat16 [65536, 8192], P(('blk', 'seq')), may hold values from -6 to 6
- seg_local: int32 [65536], P(('blk', 'seq')), may hold values from 0 to 15, as said below
- shard_counts: int32 [16, 32], P('blk', 'seq'), may hold values from 1 to 15, as said below
- norm_gain: float32 [8192], replicated, may hold values from 0.1 to 1.9
- query_weight: bfloat16 [8192, 8192], P('blk', 'seq'), may hold values from -1 to 1
- keyval_weight: bfloat16 [8192, 2, 1024], P('blk', None, 'seq'), may hold values from -4 to 4
Outputs:
- attended: bfloat16 [4096, 8192], P('blk', 'seq')
Inputs may be any that keep to these rules, and one draw needn't show every extreme that they name: Within a shard seg_local never falls and rises by at most one from token to token; it counts the segment ends before the token on that shard, so a shard's tokens after its last end continue into the next shard's segment numbered 0 there. The last token of every group ends a segment. Every shard of a group has at least one end. `shard_counts`: the number of segment ends on the shard, equal to the number of distinct seg_local values of its tokens that end there; the counts of a group sum to 256, and in every group some shard has exactly 15.
All inputs are finite; a program needn't handle non-finite values.
Results may differ from a plain program's by a relative error of at most 0.0102.
The roundings to bfloat16 on the way count: a program that leaves them out, or rounds other values in their place, can miss the bound.
Values may be sent and summed in bfloat16 or wider, within the bound.
A program may use at most 64 MiB of HBM per device.

v0:
```python
import jax
import jax.numpy as jnp
from jax import lax
from jax.sharding import PartitionSpec as P

HEAD = 128
SEG_DEV = 8


theta_base = 500000.0
norm_eps = 1e-05


def from_behind(block, axis, distance):
    devices = range(lax.axis_size(axis))
    route = [(i - distance, i) for i in devices if i - distance in devices]
    return lax.ppermute(block, axis, route)


def from_partner(value, axis, bit):
    mask = 2**bit
    pairs = [(source, source ^ mask) for source in range(lax.axis_size(axis))]
    return lax.ppermute(value, axis, pairs)


def rotate(values_in, row_pos):
    half_dim = values_in.shape[-1] // 2
    frequency = theta_base ** (
        -(jnp.arange(half_dim, dtype=jnp.float32) * 2.0 / values_in.shape[-1])
    )
    angles = row_pos.astype(jnp.float32)[:, None] * frequency[None, :]
    cosine_table = jnp.cos(angles)[:, None, :]
    sine_table = jnp.sin(angles)[:, None, :]
    front_half = values_in[..., :half_dim]
    back_half = values_in[..., half_dim:]
    return jnp.concatenate(
        [
            front_half * cosine_table - back_half * sine_table,
            back_half * cosine_table + front_half * sine_table,
        ],
        axis=-1,
    )


def on_device(tokens, seg_local, shard_counts, norm_gain, query_weight, keyval_weight):
    n_seq = lax.axis_size("seq")
    capacity = 2 * SEG_DEV - 1
    per_group = n_seq * SEG_DEV
    counts_all = lax.all_gather(shard_counts, "seq", axis=1, tiled=True)[0]
    prefix_all = jnp.cumsum(counts_all) - counts_all
    seq_pos = lax.axis_index("seq")
    chosen = jnp.arange(n_seq, dtype=jnp.int32) == seq_pos
    my_count = jnp.sum(jnp.where(chosen, counts_all, 0))
    my_start = jnp.sum(jnp.where(chosen, prefix_all, 0))
    slot_ids = jnp.arange(capacity + 1, dtype=jnp.int32)
    member = seg_local[None, :] == slot_ids[:, None]
    seg_sums = jnp.dot(member.astype(jnp.bfloat16), tokens, preferred_element_type=jnp.float32)
    seg_sizes = jnp.sum(member.astype(jnp.float32), axis=1)
    tail_sum = lax.dynamic_slice_in_dim(seg_sums, my_count, 1, 0)
    tail_size = lax.dynamic_slice_in_dim(seg_sizes, my_count, 1, 0)
    carried_sum, carried_size = from_behind((tail_sum, tail_size), "seq", 1)
    leading = slot_ids == 0
    seg_sums = seg_sums + jnp.where(leading[:, None], carried_sum, 0.0)
    seg_sizes = seg_sizes + jnp.where(leading, carried_size, 0.0)
    filled = slot_ids < my_count
    seg_means = jnp.where(
        filled[:, None], seg_sums / jnp.where(filled, seg_sizes, 1.0)[:, None], 0.0
    )
    local_rows = seg_means[:capacity].astype(jnp.bfloat16)
    rows_index = jnp.arange(per_group, dtype=jnp.int32)
    placement = (rows_index[:, None] == my_start + slot_ids[None, :capacity]) & filled[
        None, :capacity
    ]
    placed = jnp.dot(placement.astype(jnp.bfloat16), local_rows, preferred_element_type=jnp.float32)
    group_rows = lax.psum(placed.astype(jnp.bfloat16), "seq")
    widened = group_rows.astype(jnp.float32)
    normed = (
        widened
        * lax.rsqrt(jnp.mean(widened * widened, axis=-1, keepdims=True) + norm_eps)
        * norm_gain
    ).astype(jnp.bfloat16)
    query_cols = query_weight.shape[1]
    pair_cols = keyval_weight.shape[2]
    query_piece = lax.all_gather(query_weight, "blk", axis=0, tiled=True)
    pair_piece = lax.all_gather(keyval_weight, "blk", axis=0, tiled=True)
    piece_rows = query_piece.shape[0]
    query_sum = jnp.dot(normed, query_piece, preferred_element_type=jnp.float32)
    pair_sum = jnp.dot(
        normed, pair_piece.reshape(piece_rows, 2 * pair_cols), preferred_element_type=jnp.float32
    )
    query_sum, pair_sum = (query_sum, pair_sum)
    blk_pos = lax.axis_index("blk")
    positions = blk_pos * per_group + rows_index
    local_heads = query_cols // HEAD
    queries = rotate(query_sum.reshape(per_group, local_heads, HEAD), positions).astype(
        jnp.bfloat16
    )
    key_value = pair_sum.reshape(per_group, 2, pair_cols).astype(jnp.bfloat16)
    span_devices = HEAD // pair_cols
    own_pair = key_value
    for bit_number in range(span_devices.bit_length() - 1):
        partner = from_partner(own_pair, "seq", bit_number)
        upper = seq_pos // (1 << bit_number) % 2 == 1
        own_pair = jnp.where(
            upper,
            jnp.concatenate([partner, own_pair], axis=2),
            jnp.concatenate([own_pair, partner], axis=2),
        )
    own_keys = rotate(own_pair[:, 0:1].astype(jnp.float32), positions)[:, 0].astype(jnp.bfloat16)
    own_values = own_pair[:, 1]
    score_scale = float(HEAD) ** (-0.5)
    key_rows = lax.all_gather(own_keys, "blk", axis=0, tiled=True)
    value_rows = lax.all_gather(own_values, "blk", axis=0, tiled=True)
    key_pos = jnp.arange(key_rows.shape[0], dtype=jnp.int32)
    running_max = jnp.full((per_group, local_heads), -1e30, jnp.float32)
    scores = (
        jnp.einsum("qhd,kd->qhk", queries, key_rows, preferred_element_type=jnp.float32)
        * score_scale
    )
    allowed = (key_pos[None, :] <= positions[:, None])[:, None, :]
    new_max = jnp.maximum(running_max, jnp.max(jnp.where(allowed, scores, -1e30), axis=-1))
    weights = jnp.where(allowed, jnp.exp(scores - new_max[..., None]), 0.0)
    running_sum = jnp.sum(weights, axis=-1)
    mixture = jnp.einsum(
        "qhk,kd->qhd", weights.astype(jnp.bfloat16), value_rows, preferred_element_type=jnp.float32
    )
    running_max, running_sum, mixture = (new_max, running_sum, mixture)
    attended = (mixture / running_sum[..., None]).astype(jnp.bfloat16)
    return attended.reshape(per_group, local_heads * HEAD)


def solution(mesh):
    return jax.shard_map(
        on_device,
        mesh=mesh,
        in_specs=(
            P(("blk", "seq"), None),
            P(("blk", "seq")),
            P("blk", "seq"),
            P(),
            P("blk", "seq"),
            P("blk", None, "seq"),
        ),
        out_specs=P("blk", "seq"),
        check_vma=False,
    )
```

profile of v0, /device:TPU:1, one launch (start us, length us, event | category | flops | bytes accessed | tf_op | source)
XLA Modules:
  0.0 523.2 jit_solution(1895072835929042896)
XLA Ops:
  7.4 0.0 copy-start
  7.4 0.0 copy-start.2
  7.4 0.0 all-reduce.3.cloned.1.call-start
  8.2 1.3 dynamic-slice
  9.4 0.7 bitcast_dynamic-update-slice_fusion
  10.1 26.5 %all-reduce = s32[32]{0:T(128)S(1)} all-reduce(s32[32]{0:T(128)S(1)} %bitcast_dynamic-update-slice_fusion), channel_id=1, replica_groups=mesh['blk'=16,'seq'=32] {'seq'}, use_global_device_ids=true, to_apply=%add | all-reduce | flops 32 | bytes 256 | tf_op jit(solution)/shard_map/squeeze | solution.py:49
  36.7 0.1 copy.17
  36.8 0.1 reduce-window.9
  36.8 0.1 reduce
  36.9 0.7 fusion.52
  39.0 0.8 convert_reduce_fusion
  40.5 0.6 dynamic_slice.7
  41.1 2.9 collective-permute-start.1
  44.0 0.0 copy-done
  44.0 1.0 fusion.50
  45.1 3.1 collective-permute-start
  48.2 0.7 iota_compare_fusion.5
  49.0 0.7 slice_add_fusion.1
  49.6 0.0 collective-permute-done.1
  49.6 1.3 add_select_fusion
  50.9 0.0 collective-permute-done
  50.9 3.3 convolution_convert_fusion
  54.2 0.0 all-reduce.3.cloned.1.call-update
  54.2 0.0 all-gather.9.cloned.1.call-start
  54.2 0.5 all-gather.9.cloned.1.call-update
  54.8 0.0 all-gather.7.cloned.1.call-start
  54.8 0.5 all-gather.7.cloned.1.call-update
  55.4 0.0 all-gather.11.cloned.1.call-start
  55.4 330.8 %all-reduce.3.cloned.1.call-done = bf16[256,8192]{1,0:T(8,128)(2,1)} async-done(((bf16[256,8192]{1,0:T(8,128)(2,1)}), bf16[256,8192]{1,0:T(8,128)(2,1)}) %all-reduce.3.cloned.1.call-update) | async-done | bytes 4194320 | tf_op jit(solution)/shard_map/psum | solution.py:75
  386.2 3.1 fusion
  389.3 0.0 all-gather.9.cloned.1.call-done
  389.4 0.0 copy-done.2
  389.4 3.9 fusion.13
  393.3 1.9 collective-permute-start.2
  395.3 4.8 collective-permute-done.2
  400.1 1.9 collective-permute-start.3
  402.0 7.0 %collective-permute-done.3 = bf16[256,2,64]{0,2,1:T(8,128)(2,1)S(1)} collective-permute-done((bf16[256,2,64]{0,2,1:T(8,128)(2,1)S(1)}, bf16[256,2,64]{0,2,1:T(8,128)(2,1)S(1)}, u32[]{:S(2)}, u32[]{:S(2)}) %collective-permute-start.3) | collective-permute-done | bytes 65568 | tf_op jit(solution)/shard_map/ppermute | solution.py:23
  409.0 0.6 fusion.60
  409.7 0.3 fusion.45
  410.0 0.6 pad_maximum_fusion
  410.6 0.0 all-gather.11.cloned.1.call-update
  410.6 0.2 all-gather.13.cloned.1.call-start
  410.9 1.3 multiply_cosine_fusion
  412.1 0.7 iota_compare_fusion
  412.8 0.0 all-gather.13.cloned.1.call-update
  412.8 0.0 all-gather.7.cloned.1.call-done
  412.9 5.6 %fusion.11 = f32[256,256]{0,1:T(8,128)S(1)} fusion(bf16[8192,256]{1,0:T(8,128)(2,1)} %all-gather.7.cloned.1.call-done, bf16[256,8192]{1,0:T(8,128)(2,1)} %all-reduce.3.cloned.1.call-done, f32[8192]{0:T(1024)S(1)} %copy-done.2, f32[256]{0:T(256)S(1)} %add_rsqrt_fusion), kind=kOutput, calls=%fused_computation.15 | convolution fusion | flops 1082130432 | bytes 8684544 | tf_op jit(solution)/shard_map/dot_general | solution.py:87
  418.4 0.7 fusion.59
  419.1 1.0 copy.24
  420.2 0.8 copy.25
  421.0 1.8 subtract_convert_fusion
  422.8 44.9 %all-gather.11.cloned.1.call-done = bf16[4096,1,128]{0,2,1:T(8,128)(2,1)} async-done(((bf16[256,1,128]{0,2,1:T(8,128)(2,1)}), bf16[4096,1,128]{0,2,1:T(8,128)(2,1)}) %all-gather.11.cloned.1.call-update) | async-done | bytes 1048592 | tf_op jit(solution)/shard_map/all_gather | solution.py:112
  467.7 3.4 select_reduce_fusion
  471.1 0.0 copy-start.1
  471.1 3.2 copy-done.1
  474.3 2.4 fusion.3
  476.7 32.5 %all-gather.13.cloned.1.call-done = bf16[4096,1,128]{0,2,1:T(8,128)(2,1)} async-done(((bf16[256,1,128]{0,2,1:T(8,128)(2,1)}), bf16[4096,1,128]{0,2,1:T(8,128)(2,1)}) %all-gather.13.cloned.1.call-update) | async-done | bytes 1048592 | tf_op jit(solution)/shard_map/all_gather | solution.py:113
  509.1 5.6 %fusion.19 = bf16[256,2,128]{0,2,1:T(8,128)(2,1)S(1)} fusion(f32[256,2,4096]{2,0,1:T(8,128)} %copy-done.1, f32[256,2]{0,1:T(2,128)S(1)} %broadcast_maximum_fusion, pred[256,4096]{1,0:T(8,128)(4,1)S(1)} %iota_compare_fusion, bf16[4096,1,128]{0,2,1:T(8,128)(2,1)} %all-gather.13.cloned.1.call-done, f32[256,2]{0,1:T(2,128)S(1)} %fusion.3), kind=kOutput, calls=%fused_computation.18 | convolution fusion | flops 545390592 | bytes 10620928 | tf_op jit(solution)/shard_map/qhk,kd->qhd/dot_general | solution.py:124
  514.8 0.8 copy.21
  (11 shorter events, 0.1 us)
Async XLA Ops:
  7.4 36.7 %copy-start = (bf16[128,8192]{1,0:T(8,128)(2,1)S(1)}, bf16[128,8192]{1,0:T(8,128)(2,1)}, u32[]{:S(2)}) copy-start(bf16[128,8192]{1,0:T(8,128)(2,1)} %param.6) | copy-start | bytes 6291460
  7.4 382.0 %copy-start.2 = (f32[8192]{0:T(1024)S(1)}, f32[8192]{0:T(1024)}, u32[]{:S(2)}) copy-start(f32[8192]{0:T(1024)} %param.9) | copy-start | bytes 98308
  7.4 378.8 %all-reduce.3.cloned.1.call-start = ((), (), s32[]{:S(2)}) async-start(), calls=%async_computation | async-start | bytes 8388608 | tf_op jit(solution)/shard_map/psum | solution.py:75
  41.1 8.5 %collective-permute-start.1 = (f32[1]{0:T(128)}, f32[1]{0:T(128)}, u32[]{:S(2)}, u32[]{:S(2)}) collective-permute-start(f32[1]{0:T(128)} %dynamic_slice.7), channel_id=1, source_target_pairs={{0,1},{1,2},{2,3},{3,4},{4,5},{5,6},{6,7},{7,8},{8,9},{9,10},{10,1... | collective-permute-start | bytes 20 | tf_op jit(solution)/shard_map/ppermute | solution.py:17
  45.1 5.8 %collective-permute-start = (f32[1,8192]{1,0:T(1,128)S(1)}, f32[1,8192]{1,0:T(1,128)S(1)}, u32[]{:S(2)}, u32[]{:S(2)}) collective-permute-start(f32[1,8192]{1,0:T(1,128)S(1)} %constant_dynamic-slice_fusion), channel_id=1, source_target_pairs={{0,1},{1,2},{2,3},{3,4},{4,5},{5,6},{6,7},{7,8},{8,9},{9,10},{10,1... | collective-permute-start | bytes 98312 | tf_op jit(solution)/shard_map/ppermute | solution.py:17
  54.2 335.2 %all-gather.9.cloned.1.call-start = ((), (), s32[]{:S(2)}) async-start(), calls=%async_computation.2 | async-start | bytes 1114112 | tf_op jit(solution)/shard_map/all_gather | solution.py:85
  54.8 358.1 %all-gather.7.cloned.1.call-start = ((), (), s32[]{:S(2)}) async-start(), calls=%async_computation.1 | async-start | bytes 4456448 | tf_op jit(solution)/shard_map/all_gather | solution.py:84
  55.4 412.3 %all-gather.11.cloned.1.call-start = ((), (), s32[]{:S(2)}) async-start(), calls=%async_computation.3 | async-start | bytes 1114112 | tf_op jit(solution)/shard_map/all_gather | solution.py:112
  393.3 6.7 %collective-permute-start.2 = (bf16[256,2,32]{0,2,1:T(8,128)(2,1)S(1)}, bf16[256,2,32]{0,2,1:T(8,128)(2,1)S(1)}, u32[]{:S(2)}, u32[]{:S(2)}) collective-permute-start(bf16[256,2,32]{0,2,1:T(8,128)(2,1)S(1)} %fusion.13), channel_id=1, source_target_pairs={{0,1},{1,0},{2,3},{3,2},{4,5},{5,4},{6,7},{7,6},{8,9},{9,8},{10,11... | collective-permute-start | bytes 98312 | tf_op jit(solution)/shard_map/ppermute | solution.py:23
  400.1 8.9 %collective-permute-start.3 = (bf16[256,2,64]{0,2,1:T(8,128)(2,1)S(1)}, bf16[256,2,64]{0,2,1:T(8,128)(2,1)S(1)}, u32[]{:S(2)}, u32[]{:S(2)}) collective-permute-start(bf16[256,2,64]{0,2,1:T(8,128)(2,1)S(1)} %maximum_select_fusion.1), channel_id=1, source_target_pairs={{0,2},{1,3},{2,0},{3,1},{4,6},{5,7},{6,4},{7,5},{8,10},{9,11},{10,... | collective-permute-start | bytes 196616 | tf_op jit(solution)/shard_map/ppermute | solution.py:23
  410.6 98.5 %all-gather.13.cloned.1.call-start = ((), (), s32[]{:S(2)}) async-start(), calls=%async_computation.4 | async-start | bytes 1114112 | tf_op jit(solution)/shard_map/all_gather | solution.py:113
  471.1 3.2 copy-start.1
Sparse Core Ops, SparseCore 0:
  54.3 331.8 all-reduce.2
Sparse Core Ops, SparseCore 1:
  56.8 38.5 all-gather.8
  97.4 55.4 all-gather.6
  410.7 56.9 all-gather.10
  469.8 39.3 all-gather.12
where the time goes:
time: 524 us; the launch traced here: 523 us
  waiting for transfers between devices  421 us (80%)
  blocking collectives  26.5 us (5%)
  matrix products  22.8 us (4%)
  between operations  18.2 us (3%)
  other arithmetic  15.1 us (3%)
  starting transfers between devices  10.2 us (2%)
  local copies, waits for them, and re-layouts  9.19 us (2%)
    psum x1, waiting for transfers between devices, on_device(): group_rows = lax.psum(placed.astype(jnp.bfloat16), 'seq')  331 us
    all_gather x1, waiting for transfers between devices, on_device(): key_rows = lax.all_gather(own_keys, 'blk', axis=0, tiled=True)  44.9 us
    all_gather x1, waiting for transfers between devices, on_device(): value_rows = lax.all_gather(own_values, 'blk', axis=0, tiled=True)  32.5 us
    squeeze x1, blocking collectives, on_device(): counts_all = lax.all_gather(shard_counts, 'seq', axis=1, tiled=True)[0]  26.5 us
    ppermute x2, waiting for transfers between devices, from_partner(): return lax.ppermute(value, axis, pairs)  11.7 us
  transfers between devices with their start and end apart: 9, of which 5 were waited for; matrix products, arithmetic and copies ran while one was open for 6% of the time, Pallas kernels for 0%

commit v1 on v0

v1 whole, which is shorter than its diff:
```python
import jax
import jax.numpy as jnp
from jax import lax
from jax.experimental import pallas as pl
from jax.experimental.pallas import tpu as pltpu
from jax.sharding import PartitionSpec as P

HEAD = 128
SLOTS = 16
COLS = 256
NZ, NY = 8, 4
NX, NYL, NC = 4, 2, 2
N_SEQ = NZ * NY
N_BLK = NYL * NX * NC
THETA = 500000.0
EPS = 1e-05
F32 = jnp.float32
BF16 = jnp.bfloat16


def rdma(src, dst, send, recv, where):
    return pltpu.make_async_remote_copy(
        src_ref=src, dst_ref=dst, send_sem=send, recv_sem=recv,
        device_id=where, device_id_type=pl.DeviceIdType.MESH,
    )


def blk_parts():
    blk = lax.axis_index("blk")
    return blk, blk // (NX * NC), (blk // NC) % NX, blk % NC


def blk_of(yl, x, c):
    return (yl * NX + x % NX) * NC + c


class PlaneGather:
    def __init__(self, buf, send, recv):
        self.buf, self.send, self.recv = buf, send, recv
        self.blk, self.yl, self.x, self.c = blk_parts()
        self.started = []

    def peers(self):
        return [
            blk_of(self.yl, self.x + 1, self.c), blk_of(self.yl, self.x + 3, self.c),
            blk_of(1 - self.yl, self.x, self.c), blk_of(self.yl, self.x, 1 - self.c),
        ]

    def move(self, sem, kind, dx, target):
        yl = self.yl if kind == 0 else 1 - self.yl
        origin = blk_of(yl, self.x + dx, self.c)
        copy = rdma(self.buf.at[origin], self.buf.at[origin], self.send.at[sem],
                    self.recv.at[sem], {"blk": target})
        copy.start()
        self.started.append(copy)

    def east(self, sem, kind, dx):
        self.move(sem, kind, dx, blk_of(self.yl, self.x + 1, self.c))

    def west(self, sem, kind, dx):
        self.move(sem, kind, dx, blk_of(self.yl, self.x + 3, self.c))

    def core(self, sem, kind, dx):
        self.move(sem, kind, dx, blk_of(self.yl, self.x, 1 - self.c))

    def arrive(self, sem):
        rdma(self.buf.at[0], self.buf.at[0], self.send.at[sem], self.recv.at[sem],
             {"blk": self.blk}).wait_recv()

    def phase0(self):
        self.east(1, 0, 0)
        self.west(2, 0, 0)
        self.core(7, 0, 0)

    def pair(self):
        self.move(0, 0, 0, blk_of(1 - self.yl, self.x, self.c))

    def phase1(self):
        self.arrive(1)
        self.east(3, 0, -1)
        self.core(8, 0, -1)
        self.arrive(2)
        self.core(9, 0, 1)

    def phase2(self):
        self.arrive(0)
        self.east(4, 1, 0)
        self.west(5, 1, 0)
        self.core(10, 1, 0)
        self.arrive(3)
        self.core(11, 0, 2)

    def phase3(self):
        self.arrive(5)
        self.west(6, 1, 1)
        self.core(12, 1, 1)
        self.arrive(4)
        self.core(13, 1, -1)

    def phase4(self):
        self.arrive(6)
        self.core(14, 1, 2)

    def finish(self):
        for sem in range(7, 15):
            self.arrive(sem)
        for copy in self.started:
            copy.wait_send()


def mm(a, b, dims=((1,), (0,))):
    return lax.dot_general(a, b, (dims, ((), ())), preferred_element_type=F32)


def iota(shape, axis):
    return lax.broadcasted_iota(jnp.int32, shape, axis)


def project_kernel(
    tokens, seg, count, weight, gain, cosine, sine, q_out, kv_out,
    main, extra, got_main, got_extra, rows, wbuf, squares, acc_q, acc_kv,
    a2a_send, a2a_recv, y_send, y_recv, z_send, z_recv, w_send, w_recv, local_sem,
):
    me = lax.axis_index("seq")
    z, y = me // NY, me % NY
    gather = PlaneGather(wbuf, w_send, w_recv)
    turn = 1 - 2 * gather.c

    def seq_of(zz, yy):
        return ((zz + 2 * NZ) % NZ) * NY + (yy + 2 * NY) % NY

    barrier = pltpu.get_barrier_semaphore()

    def greet(k, carry):
        pl.semaphore_signal(barrier, inc=1, device_id={"seq": (me + k) % N_SEQ},
                            device_id_type=pl.DeviceIdType.MESH)
        return carry

    lax.fori_loop(1, N_SEQ, greet, 0)
    for peer in gather.peers():
        pl.semaphore_signal(barrier, inc=1, device_id={"blk": peer},
                            device_id_type=pl.DeviceIdType.MESH)

    own_weight = pltpu.make_async_copy(weight, wbuf.at[gather.blk], local_sem)
    own_weight.start()

    slot = iota((SLOTS, 128), 0)
    member = (seg[...] == slot).astype(F32)
    sizes = jnp.sum(member, axis=1, keepdims=True)
    member = member.astype(BF16)
    is_tail = (slot == count[...]).astype(F32)
    tail_pick = is_tail[:, 0:1]
    tail_size = jnp.sum(sizes * is_tail, axis=0, keepdims=True)
    safe = jnp.maximum(sizes, 1.0)
    count_row = count[...].astype(F32)
    lead_size = jnp.broadcast_to(sizes[0:1], (1, 128))

    def pool(d, carry):
        column = pl.multiple_of(d * COLS, COLS)
        sums = mm(member, tokens[:, pl.ds(column, COLS)])
        main[d] = (sums / safe).astype(BF16)
        tail = jnp.sum(sums * tail_pick, axis=0, keepdims=True)
        extra[d] = jnp.concatenate(
            [sums[0:1, :128], sums[0:1, 128:], tail[:, :128], tail[:, 128:],
             count_row, lead_size, tail_size, jnp.zeros((1, 128), F32)], axis=0)
        return carry

    lax.fori_loop(0, N_SEQ, pool, 0)
    got_extra[0] = jnp.zeros((8, 128), F32)
    pl.semaphore_wait(barrier, N_SEQ - 1 + 4)

    def exchange(k):
        to = (me + k) % N_SEQ
        return (
            rdma(main.at[to], got_main.at[me], a2a_send.at[0, k], a2a_recv.at[0, k], {"seq": to}),
            rdma(extra.at[to], got_extra.at[me + 1], a2a_send.at[1, k], a2a_recv.at[1, k],
                 {"seq": to}),
        )

    def send_one(k, carry):
        for copy in exchange(k):
            copy.start()
        return carry

    def land_one(k, carry):
        for copy in exchange(k):
            copy.wait_recv()
        return carry

    def drain_one(k, carry):
        for copy in exchange(k):
            copy.wait_send()
        return carry

    lax.fori_loop(1, N_SEQ, send_one, 0)
    own_weight.wait()
    gather.phase0()
    got_main[me] = main[me]
    got_extra[me + 1] = extra[me]
    lax.fori_loop(1, N_SEQ, land_one, 0)

    total = N_SEQ * SLOTS
    counts = got_extra[1:N_SEQ + 1, 4, :]
    source = iota((N_SEQ, total), 0)
    owner = iota((N_SEQ, total), 1) // SLOTS
    counts16 = counts.astype(BF16)
    before = mm(counts16, (source < owner).astype(BF16), ((0,), (0,)))
    inside = mm(counts16, (source == owner).astype(BF16), ((0,), (0,)))
    rank = (iota((128, total), 1) % SLOTS).astype(F32)
    lead_sizes = got_extra[1:N_SEQ + 1, 5, :] + got_extra[0:N_SEQ, 6, :]
    border = jnp.concatenate(
        [(got_extra[1:N_SEQ + 1, i, :] + got_extra[0:N_SEQ, 2 + i, :]) / lead_sizes
         for i in range(2)], axis=1).astype(BF16)
    spread = (iota((total, N_SEQ), 0) // SLOTS == iota((total, N_SEQ), 1)).astype(BF16)
    slots = got_main[...].reshape(total, COLS)
    first = iota((total, COLS), 0) % SLOTS == 0
    slots = jnp.where(first, mm(spread, border), slots.astype(F32)).astype(BF16)
    for half in range(2):
        row = (iota((128, total), 0) + 128 * half).astype(F32)
        place = jnp.where(rank < inside, (before + rank == row).astype(F32), 0.0).astype(BF16)
        rows[me, pl.ds(128 * half, 128), :] = mm(place, slots).astype(BF16)

    lax.fori_loop(1, N_SEQ, drain_one, 0)

    started = []

    def y_step(sem, origin, step):
        copy = rdma(rows.at[origin], rows.at[origin], y_send.at[sem], y_recv.at[sem],
                    {"seq": seq_of(z, y + step)})
        copy.start()
        started.append(copy)

    def y_arrive(sem):
        rdma(rows.at[0], rows.at[0], y_send.at[sem], y_recv.at[sem], {"seq": me}).wait_recv()

    origin_y = (y, y - turn, y + turn, y + 2)
    hops = ((4, 3), (3, 4), (4, 3), (3, 4))

    def z_step(j, h):
        for side, step in ((0, 1), (1, -1)):
            if h < hops[j][side]:
                sem = (side * 4 + j) * 4 + h
                if h > 0:
                    z_arrive(j, h - 1, side)
                origin = seq_of(z - step * h, origin_y[j])
                copy = rdma(rows.at[origin], rows.at[origin], z_send.at[sem], z_recv.at[sem],
                            {"seq": seq_of(z + step, y)})
                copy.start()
                started.append(copy)

    def z_arrive(j, h, side):
        sem = (side * 4 + j) * 4 + h
        rdma(rows.at[0], rows.at[0], z_send.at[sem], z_recv.at[sem], {"seq": me}).wait_recv()

    z_step(0, 0)
    y_step(0, me, turn)
    y_step(1, me, -turn)
    gather.phase1()
    y_arrive(0)
    y_step(2, seq_of(z, y - turn), turn)
    z_step(1, 0)
    gather.pair()
    y_arrive(1)
    z_step(2, 0)
    z_step(0, 1)
    y_arrive(2)
    z_step(3, 0)
    z_step(1, 1)
    z_step(2, 1)
    gather.phase2()
    z_step(0, 2)
    z_step(3, 1)
    z_step(1, 2)
    gather.phase3()
    z_step(2, 2)
    z_step(3, 2)
    z_step(0, 3)
    gather.phase4()
    z_step(1, 3)
    z_step(2, 3)
    z_step(3, 3)
    gather.finish()
    for j in range(4):
        for side in range(2):
            z_arrive(j, hops[j][side] - 1, side)

    squares[...] = jnp.zeros_like(squares)

    def square(d, carry):
        piece = rows[d].astype(F32)
        squares[...] += piece * piece
        return carry

    lax.fori_loop(0, N_SEQ, square, 0)
    mean = jnp.sum(squares[...], axis=1, keepdims=True) * (1.0 / (N_SEQ * COLS))
    scale = lax.rsqrt(mean + EPS)
    acc_q[...] = jnp.zeros_like(acc_q)
    acc_kv[...] = jnp.zeros_like(acc_kv)

    def multiply(p, carry):
        for half in range(2):
            d = 2 * p + half
            normed = (rows[d].astype(F32) * scale * gain[pl.ds(d, 1), :]).astype(BF16)
            acc_q[...] += mm(normed, wbuf[p, pl.ds(256 * half, 256), :])
            acc_kv[...] += mm(wbuf[p, pl.ds(512 + 64 * half, 64), :], normed, ((1,), (1,)))
        return carry

    lax.fori_loop(0, N_BLK, multiply, 0)
    for head in range(2):
        one = acc_q[:, pl.ds(HEAD * head, HEAD)]
        turned = one * cosine[...] + pltpu.roll(one, HEAD // 2, 1) * sine[...]
        q_out[:, pl.ds(HEAD * head, HEAD)] = turned.astype(BF16)
    kv_out[...] = acc_kv[...].astype(BF16)
    for copy in started:
        copy.wait_send()


def spread_kernel(kv, cosine, sine, out, parts, q_send, q_recv, p_send, p_recv):
    me = lax.axis_index("seq")
    z, y = me // NY, me % NY
    gather = PlaneGather(out, p_send, p_recv)
    barrier = pltpu.get_barrier_semaphore()
    for k in range(1, NY):
        pl.semaphore_signal(barrier, inc=1, device_id={"seq": z * NY + (y + k) % NY},
                            device_id_type=pl.DeviceIdType.MESH)
    for peer in gather.peers():
        pl.semaphore_signal(barrier, inc=1, device_id={"blk": peer},
                            device_id_type=pl.DeviceIdType.MESH)
    pl.semaphore_wait(barrier, NY - 1 + 4)
    copies = [
        rdma(kv, parts.at[y], q_send.at[k], q_recv.at[k], {"seq": z * NY + (y + k) % NY})
        for k in range(1, NY)
    ]
    for copy in copies:
        copy.start()
    parts[y] = kv[...]
    for copy in copies:
        copy.wait()
    keys = jnp.concatenate([parts[i, pl.ds(0, 32), :] for i in range(NY)], axis=0).astype(F32)
    low, high = keys[:64], keys[64:]
    cos, sin = cosine[...], sine[...]
    mine = gather.blk
    out[mine, pl.ds(0, 64), :] = (low * cos - high * sin).astype(BF16)
    out[mine, pl.ds(64, 64), :] = (high * cos + low * sin).astype(BF16)
    for i in range(NY):
        out[mine, pl.ds(128 + 32 * i, 32), :] = parts[i, pl.ds(32, 32), :]
    gather.pair()
    gather.phase0()
    gather.phase1()
    gather.phase2()
    gather.phase3()
    gather.phase4()
    gather.finish()


def attend_kernel(q, kv, out, scores, peak, total, acc):
    blk = lax.axis_index("blk")
    unit = float(HEAD) ** (-0.5)
    for head in range(2):
        query = q[:, pl.ds(HEAD * head, HEAD)]
        peak[...] = jnp.full_like(peak, -1e30)

        def score(g, carry):
            s = mm(query, kv[g, pl.ds(0, HEAD), :]) * unit
            ok = g * 256 + iota((256, 256), 1) <= blk * 256 + iota((256, 256), 0)
            s = jnp.where(ok, s, -1e30)
            scores[g] = s
            peak[...] = jnp.maximum(peak[...], s)
            return carry

        lax.fori_loop(0, blk + 1, score, 0)
        top = jnp.max(peak[...], axis=1, keepdims=True)
        total[...] = jnp.zeros_like(total)
        acc[...] = jnp.zeros_like(acc)

        def mix(g, carry):
            w = jnp.exp(scores[g] - top)
            total[...] += w
            acc[...] += mm(w.astype(BF16), kv[g, pl.ds(HEAD, HEAD), :], ((1,), (1,)))
            return carry

        lax.fori_loop(0, blk + 1, mix, 0)
        norm = jnp.sum(total[...], axis=1, keepdims=True)
        out[:, pl.ds(HEAD * head, HEAD)] = (acc[...] / norm).astype(BF16)


def on_device(tokens, seg_local, shard_counts, norm_gain, query_weight, keyval_weight):
    rows_in_group = N_SEQ * 8
    vmem = pl.BlockSpec(memory_space=pltpu.VMEM)
    dma = pltpu.SemaphoreType.DMA
    blk = lax.axis_index("blk")
    positions = (blk * rows_in_group + jnp.arange(rows_in_group, dtype=jnp.int32)).astype(F32)
    half = HEAD // 2
    frequency = THETA ** (-(jnp.arange(half, dtype=F32) * 2.0 / HEAD))
    angles = positions[:, None] * frequency[None, :]
    cos, sin = jnp.cos(angles), jnp.sin(angles)
    cos2 = jnp.concatenate([cos, cos], axis=1)
    sin2 = jnp.concatenate([-sin, sin], axis=1)
    kv_t = keyval_weight.reshape(512, 64).T
    weight = jnp.concatenate([query_weight, kv_t[:, :256], kv_t[:, 256:]], axis=0)
    gain = norm_gain.reshape(N_SEQ, COLS)
    count = jnp.broadcast_to(shard_counts, (1, 128))
    q, kv = pl.pallas_call(
        project_kernel,
        out_shape=(
            jax.ShapeDtypeStruct((256, 256), BF16),
            jax.ShapeDtypeStruct((64, 256), BF16),
        ),
        in_specs=[vmem] * 7,
        out_specs=(vmem, vmem),
        scratch_shapes=[
            pltpu.VMEM((N_SEQ, SLOTS, COLS), BF16),
            pltpu.VMEM((N_SEQ, 8, 128), F32),
            pltpu.VMEM((N_SEQ, SLOTS, COLS), BF16),
            pltpu.VMEM((N_SEQ + 1, 8, 128), F32),
            pltpu.VMEM((N_SEQ, 256, COLS), BF16),
            pltpu.VMEM((N_BLK, 640, 256), BF16),
            pltpu.VMEM((256, COLS), F32),
            pltpu.VMEM((256, 256), F32),
            pltpu.VMEM((64, 256), F32),
            dma((2, N_SEQ)), dma((2, N_SEQ)),
            dma((3,)), dma((3,)),
            dma((32,)), dma((32,)),
            dma((15,)), dma((15,)),
            dma,
        ],
        compiler_params=pltpu.CompilerParams(
            collective_id=0, has_side_effects=True, vmem_limit_bytes=40 << 20),
        name="project",
    )(tokens, seg_local.reshape(1, 128), count, weight, gain, cos2, sin2)
    pieces = pl.pallas_call(
        spread_kernel,
        out_shape=jax.ShapeDtypeStruct((N_BLK, 256, 256), BF16),
        in_specs=[vmem] * 3,
        out_specs=vmem,
        scratch_shapes=[
            pltpu.VMEM((NY, 64, 256), BF16),
            dma((NY,)), dma((NY,)),
            dma((15,)), dma((15,)),
        ],
        compiler_params=pltpu.CompilerParams(
            collective_id=1, has_side_effects=True, vmem_limit_bytes=16 << 20),
        name="spread",
    )(kv, cos.T, sin.T)
    return pl.pallas_call(
        attend_kernel,
        out_shape=jax.ShapeDtypeStruct((256, 256), BF16),
        in_specs=[vmem] * 2,
        out_specs=vmem,
        scratch_shapes=[
            pltpu.VMEM((N_BLK, 256, 256), F32),
            pltpu.VMEM((256, 256), F32),
            pltpu.VMEM((256, 256), F32),
            pltpu.VMEM((256, HEAD), F32),
        ],
        compiler_params=pltpu.CompilerParams(vmem_limit_bytes=24 << 20),
        name="attend",
    )(q, pieces)


def solution(mesh):
    return jax.shard_map(
        on_device,
        mesh=mesh,
        in_specs=(
            P(("blk", "seq"), None),
            P(("blk", "seq")),
            P("blk", "seq"),
            P(),
            P("blk", "seq"),
            P("blk", None, "seq"),
        ),
        out_specs=P("blk", "seq"),
        check_vma=False,
    )
```

time: 524 us -> 126 us (0.24)
  the two profiles are of different devices: /device:TPU:1 before, /device:TPU:15 now
where the time goes in v1:
time: 126 us
  Pallas kernels  119 us (94%)
  local copies, waits for them, and re-layouts  3.8 us (3%)
  other arithmetic  1.96 us (2%)
    pallas_call x1, Pallas kernels, on_device(): pl.pallas_call(project_kernel, out_shape=(jax.ShapeDtypeStruct((256, 256)...  79.6 us
    pallas_call x1, Pallas kernels, on_device(): pl.pallas_call(spread_kernel, out_shape=jax.ShapeDtypeStruct((N_BLK, 256,...  26.6 us
    pallas_call x1, Pallas kernels, on_device(): pl.pallas_call(attend_kernel, out_shape=jax.ShapeDtypeStruct((256, 256),...  13.2 us

profile of v1, /device:TPU:15, one launch (start us, length us, event | category | flops | bytes accessed | tf_op | source)
XLA Modules:
  0.0 125.8 jit_solution(14507474586171079089)
XLA Ops:
  0.7 0.8 reshape.24.gain
  1.5 0.8 fusion.1
  2.2 0.3 multiply_sine_fusion.1
  2.6 1.0 pad_maximum_fusion.weight
  3.5 0.5 fusion
  4.1 0.1 pad_maximum_fusion.1
  4.2 0.0 copy-start
  4.2 1.6 %copy-done = bf16[128,8192]{1,0:T(8,128)(2,1)S(1)} copy-done((bf16[128,8192]{1,0:T(8,128)(2,1)S(1)}, bf16[128,8192]{1,0:T(8,128)(2,1)}, u32[]{:S(2)}) %copy-start) | copy-done | bytes 2097176
  5.8 0.0 copy-start.1
  5.8 0.7 copy-done.1
  6.5 79.6 %project.1 = (bf16[256,256]{1,0:T(8,128)(2,1)S(1)}, bf16[64,256]{1,0:T(8,128)(2,1)S(1)}) custom-call(bf16[128,8192]{1,0:T(8,128)(2,1)S(1)} %copy-done, s32[1,128]{1,0:T(1,128)S(1)} %bitcast.6, s32[1,128]{1,0:T(1,128)S(1)} %broadcast_in_dim.10.count, bf16[640,256]{1,0:T(8,128)(2,1)S(1)} %pad_maximum_fusion.weight, f32[32,256]{1,0:T(8,128)S(1)} %reshape.24.gain, ...), custom_call_target="tpu_custom_call" | custom-call | tf_op jit(solution)/shard_map/project/pallas_call | solution.py:403
  86.0 26.6 %spread.1.kv = bf16[16,256,256]{2,1,0:T(8,128)(2,1)S(1)} custom-call(bf16[64,256]{1,0:T(8,128)(2,1)S(1)} %get-tuple-element.8.kv, f32[64,256]{1,0:T(8,128)S(1)} %get-tuple-element.12.cosine, f32[64,256]{1,0:T(8,128)S(1)} %get-tuple-element.11.sine), custom_call_target="tpu_custom_call" | custom-call | tf_op jit(solution)/shard_map/spread/pallas_call | solution.py:431
  112.6 13.2 %attend.1 = bf16[256,256]{1,0:T(8,128)(2,1)} custom-call(bf16[256,256]{1,0:T(8,128)(2,1)S(1)} %get-tuple-element.7.q, bf16[16,256,256]{2,1,0:T(8,128)(2,1)S(1)} %spread.1.kv), custom_call_target="tpu_custom_call" | custom-call | tf_op jit(solution)/shard_map/attend/pallas_call | solution.py:445
  (3 shorter events, 0.0 us)
Async XLA Ops:
  4.2 1.6 %copy-start = (bf16[128,8192]{1,0:T(8,128)(2,1)S(1)}, bf16[128,8192]{1,0:T(8,128)(2,1)}, u32[]{:S(2)}) copy-start(bf16[128,8192]{1,0:T(8,128)(2,1)} %tokens.1) | copy-start | bytes 6291460
  5.8 0.7 copy-start.1

commit v2 on v0

v2 whole, which is shorter than its diff:
```python
import heapq

import jax
import jax.numpy as jnp
from jax import lax
from jax.experimental import pallas as pl
from jax.experimental.pallas import tpu as pltpu
from jax.sharding import PartitionSpec as P

HEAD = 128
SLOTS = 16
COLS = 256
NZ, NY = 8, 4
NX, NYL, NC = 4, 2, 2
N_SEQ = NZ * NY
N_BLK = NYL * NX * NC
UPPER = 176
THETA = 500000.0
EPS = 1e-05
F32 = jnp.float32
BF16 = jnp.bfloat16
MESH = pl.DeviceIdType.MESH


class Stream:
    def __init__(self, name, link, cost, lag, parent, make, group, delay=0.0):
        self.name, self.link, self.cost, self.lag = name, link, cost, lag
        self.parent, self.make, self.group, self.delay = parent, make, group, delay
        self.begun = False

    def start(self, started):
        self.begun = True
        copy = self.make()
        copy.start()
        started.append(copy)

    def arrive(self):
        self.make().wait_recv()


def schedule(streams):
    by_name = {s.name: i for i, s in enumerate(streams)}
    children = {i: [] for i in range(len(streams))}
    heap, actions = [], []
    for i, s in enumerate(streams):
        if s.parent is None:
            heap.append((s.delay, i))
        else:
            children[by_name[s.parent]].append(i)
    heapq.heapify(heap)
    free = {}
    while heap:
        ready, i = heapq.heappop(heap)
        s = streams[i]
        if s.parent is None and s.delay > 0.0:
            actions.append((ready, 0, i))
        end = max(ready, free.get(s.link, 0.0)) + s.cost
        free[s.link] = end
        actions.append((end + s.lag, 1, i))
        for c in children[i]:
            heapq.heappush(heap, (end + s.lag, c))
    return sorted(actions), children


def run(streams, started, after):
    actions, children = schedule(streams)
    for k, (time, kind, i) in enumerate(actions):
        if kind == 0:
            if not streams[i].begun:
                streams[i].start(started)
            continue
        streams[i].arrive()
        for c in children[i]:
            streams[c].start(started)
        later = [t for t, kd, j in actions[k + 1:] if kd == 0 or children[j]]
        after(streams[i], time, later[0] if later else None)


def rdma(src, dst, send, recv, where):
    return pltpu.make_async_remote_copy(
        src_ref=src, dst_ref=dst, send_sem=send, recv_sem=recv,
        device_id=where, device_id_type=MESH,
    )


def blk_parts():
    blk = lax.axis_index("blk")
    return blk, blk // (NX * NC), (blk // NC) % NX, blk % NC


def blk_of(yl, x, c):
    return (yl * NX + (x + NX) % NX) * NC + c


def plane_peers():
    _, yl, x, c = blk_parts()
    return [blk_of(yl, x + 1, c), blk_of(yl, x - 1, c), blk_of(1 - yl, x, c), blk_of(yl, x, 1 - c)]


PLANE = (
    ("east0", "east", None, 0, 0, 0),
    ("west0", "west", None, 0, 0, 1),
    ("core0", "core", None, 0, 0, 3),
    ("pair", "pair", None, 0, 0, 2),
    ("east1", "east", "east0", 0, -1, 0),
    ("core1", "core", "east0", 0, -1, 3),
    ("core2", "core", "west0", 0, 1, 3),
    ("core3", "core", "east1", 0, 2, 3),
    ("east2", "east", "pair", 1, 0, 0),
    ("west2", "west", "pair", 1, 0, 1),
    ("core4", "core", "pair", 1, 0, 3),
    ("west3", "west", "west2", 1, 1, 1),
    ("core5", "core", "west2", 1, 1, 3),
    ("core6", "core", "east2", 1, -1, 3),
    ("core7", "core", "west3", 1, 2, 3),
)
LANDS = {
    "east0": (0, -1, 0), "west0": (0, 1, 0), "core0": (0, 0, 1), "pair": (1, 0, 0),
    "east1": (0, 2, 0), "core1": (0, -1, 1), "core2": (0, 1, 1), "core3": (0, 2, 1),
    "east2": (1, -1, 0), "west2": (1, 1, 0), "core4": (1, 0, 1), "west3": (1, 2, 0),
    "core5": (1, 1, 1), "core6": (1, -1, 1), "core7": (1, 2, 1),
}


def plane_streams(buf, send, recv, cost, parts, group, pair_delay):
    _, yl, x, c = blk_parts()
    targets = plane_peers()
    streams = []
    for p, (first, size) in enumerate(parts):
        for i, (name, link, parent, kind, dx, target) in enumerate(PLANE):
            origin = blk_of(yl if kind == 0 else 1 - yl, x + dx, c)
            piece = buf.at[origin, pl.ds(first, size)]
            sem = p * len(PLANE) + i

            def make(piece=piece, sem=sem, target=target):
                return rdma(piece, piece, send.at[sem], recv.at[sem], {"blk": targets[target]})

            streams.append(Stream(
                (name, p), link, cost / 5 if link == "core" else cost,
                1.0 if link == "core" else 1.7, None if parent is None else (parent, p), make,
                (group, name), pair_delay if name == "pair" else 0.0))
    return streams


def mm(a, b, dims=((1,), (0,))):
    return lax.dot_general(a, b, (dims, ((), ())), preferred_element_type=F32)


def iota(shape, axis):
    return lax.broadcasted_iota(jnp.int32, shape, axis)


def layer_kernel(
    tokens, seg, count, q_weight, kv_weight, gain, cosine, sine, cos_t, sin_t, out,
    tok, main, extra, got_main, got_extra, sq, got_sq, rows, wbuf, scale, acc_q, acc_kv,
    query, kv, parts, keys, top, total, acc,
    tok_sem, own_sem, a2a_send, a2a_recv, sq_send, sq_recv, r_send, r_recv,
    w_send, w_recv, quad_send, quad_recv, k_send, k_recv,
):
    me = lax.axis_index("seq")
    z, y = me // NY, me % NY
    blk, yl, x, core = blk_parts()
    turn = 1 - 2 * core

    def seq_of(zz, yy):
        return ((zz + 2 * NZ) % NZ) * NY + (yy + 2 * NY) % NY

    barrier = pltpu.get_barrier_semaphore()

    def greet(k, carry):
        pl.semaphore_signal(barrier, inc=1, device_id={"seq": (me + k) % N_SEQ},
                            device_id_type=MESH)
        return carry

    chunk = N_SEQ * COLS // 4
    token_loads = [
        pltpu.make_async_copy(tokens.at[:, pl.ds(i * chunk, chunk)],
                              tok.at[:, pl.ds(i * chunk, chunk)], tok_sem.at[i])
        for i in range(4)
    ]
    own_loads = [
        pltpu.make_async_copy(q_weight, wbuf.at[blk, pl.ds(0, 512)], own_sem.at[0]),
        pltpu.make_async_copy(kv_weight.at[:, pl.ds(0, 256)], wbuf.at[blk, pl.ds(512, 64)],
                              own_sem.at[1]),
        pltpu.make_async_copy(kv_weight.at[:, pl.ds(256, 256)], wbuf.at[blk, pl.ds(576, 64)],
                              own_sem.at[2]),
    ]
    for load in token_loads + own_loads:
        load.start()
    lax.fori_loop(1, N_SEQ, greet, 0)
    for peer in plane_peers():
        pl.semaphore_signal(barrier, inc=1, device_id={"blk": peer}, device_id_type=MESH)

    slot = iota((SLOTS, 128), 0)
    member = (seg[...] == slot).astype(F32)
    sizes = jnp.sum(member, axis=1, keepdims=True)
    member = member.astype(BF16)
    is_tail = (slot == count[...]).astype(F32)
    tail_pick = is_tail[:, 0:1]
    tail_size = jnp.sum(sizes * is_tail, axis=0, keepdims=True)
    safe = jnp.maximum(sizes, 1.0)
    count_row = count[...].astype(F32)
    lead_size = jnp.broadcast_to(sizes[0:1], (1, 128))

    def pool(d, carry):
        column = pl.multiple_of(d * COLS, COLS)
        sums = mm(member, tok[:, pl.ds(column, COLS)])
        main[d] = (sums / safe).astype(BF16)
        tail = jnp.sum(sums * tail_pick, axis=0, keepdims=True)
        extra[d] = jnp.concatenate(
            [sums[0:1, :128], sums[0:1, 128:], tail[:, :128], tail[:, 128:],
             count_row, lead_size, tail_size, jnp.zeros((1, 128), F32)], axis=0)
        return carry

    for i in range(4):
        token_loads[i].wait()
        lax.fori_loop(8 * i, 8 * i + 8, pool, 0)
    got_extra[0] = jnp.zeros((8, 128), F32)
    for load in own_loads:
        load.wait()
    pl.semaphore_wait(barrier, N_SEQ - 1 + 4)

    def exchange(k):
        to = (me + k) % N_SEQ
        return (
            rdma(main.at[to], got_main.at[me], a2a_send.at[0, k], a2a_recv.at[0, k], {"seq": to}),
            rdma(extra.at[to], got_extra.at[me + 1], a2a_send.at[1, k], a2a_recv.at[1, k],
                 {"seq": to}),
        )

    def share(k):
        return (rdma(sq, got_sq.at[me], sq_send.at[k], sq_recv.at[k], {"seq": (me + k) % N_SEQ}),)

    def each(copies, what):
        def body(k, carry):
            for copy in copies(k):
                getattr(copy, what)()
            return carry

        lax.fori_loop(1, N_SEQ, body, 0)

    started = []
    weights = plane_streams(wbuf, w_send, w_recv, 7.3, ((0, 640),), "weight", 12.0)
    each(exchange, "start")
    for s in weights:
        if s.parent is None and s.delay == 0.0:
            s.start(started)
    got_main[me] = main[me]
    got_extra[me + 1] = extra[me]
    each(exchange, "wait_recv")

    slots_all = N_SEQ * SLOTS
    counts16 = got_extra[1:N_SEQ + 1, 4, :].astype(BF16)
    source = iota((N_SEQ, slots_all), 0)
    owner = iota((N_SEQ, slots_all), 1) // SLOTS
    before = mm(counts16, (source < owner).astype(BF16), ((0,), (0,)))
    inside = mm(counts16, (source == owner).astype(BF16), ((0,), (0,)))
    rank = (iota((128, slots_all), 1) % SLOTS).astype(F32)
    lead_sizes = got_extra[1:N_SEQ + 1, 5, :] + got_extra[0:N_SEQ, 6, :]
    border = jnp.concatenate(
        [(got_extra[1:N_SEQ + 1, i, :] + got_extra[0:N_SEQ, 2 + i, :]) / lead_sizes
         for i in range(2)], axis=1).astype(BF16)
    spread = (iota((slots_all, N_SEQ), 0) // SLOTS == iota((slots_all, N_SEQ), 1)).astype(BF16)
    slots = got_main[...].reshape(slots_all, COLS)
    first = iota((slots_all, COLS), 0) % SLOTS == 0
    slots = jnp.where(first, mm(spread, border), slots.astype(F32)).astype(BF16)
    ones = jnp.ones((8, COLS), BF16)
    for half in range(2):
        row = (iota((128, slots_all), 0) + 128 * half).astype(F32)
        place = jnp.where(rank < inside, (before + rank == row).astype(F32), 0.0).astype(BF16)
        rows[me, pl.ds(128 * half, 128), :] = mm(place, slots).astype(BF16)
    for half in range(2):
        piece = rows[me, pl.ds(128 * half, 128), :].astype(F32)
        square = piece * piece
        coarse = square.astype(BF16)
        fine = (square - coarse.astype(F32)).astype(BF16)
        across = mm(ones, coarse, ((1,), (1,))) + mm(ones, fine, ((1,), (1,)))
        sq[half:half + 1, :] = across[0:1]

    streams = list(weights)
    counter = [0]

    def add(name, link, cost, lag, parent, part, origin, target, group):
        sem = counter[0]
        counter[0] += 1
        at, size = ((0, UPPER), (UPPER, 256 - UPPER))[part]
        piece = rows.at[seq_of(z + origin[0], y + origin[1]), pl.ds(at, size)]
        where = {"seq": seq_of(z + target[0], y + target[1])}

        def make():
            return rdma(piece, piece, r_send.at[sem], r_recv.at[sem], where)

        streams.append(Stream(name, link, cost, lag, parent, make, ("row", group),
                              13.0 if parent is None else 0.0))

    zc, yc = (2.0, 0.95), (2.0, 0.95)
    dys = (0, -turn, turn, 2)
    hops = ((4, 3), (3, 4), (4, 3), (3, 4))
    own = ("yA", "yB", "yC")

    def z_upper(j, h):
        for side, step in ((0, 1), (1, -1)):
            if h < hops[j][side]:
                parent = ("z", j, side, h - 1) if h else (None if j == 0 else own[j - 1])
                add(("z", j, side, h), "z%d" % side, zc[0], 1.7, parent, 0,
                    (-step * h, dys[j]), (step, 0), h + 1)

    def y_all(tag, parent, part, dz, group):
        names = own if tag is None else tuple((n, tag) for n in own)
        add(names[0], "y", yc[part], 2.4, parent, part, (dz, 0), (0, turn), group)
        add(names[1], "y", yc[part], 2.4, parent, part, (dz, 0), (0, -turn), group)
        add(names[2], "y", yc[part], 2.4, names[0], part, (dz, -turn), (0, turn), group)

    z_upper(0, 0)
    y_all(None, None, 0, 0, 0)
    for side, step in ((0, turn), (1, -turn)):
        for h in range((4, 3)[side]):
            add(("zz", side, h), "z%d" % side, zc[1], 1.7, ("zz", side, h - 1) if h else None, 1,
                (-step * h, 0), (step, 0), h + 1)
            y_all(("zz", side, h), ("zz", side, h), 1, -step * (h + 1), h + 1)
    y_all("zz", None, 1, 0, 0)
    for h in range(4):
        for j in range(4):
            if (j, h) != (0, 0):
                z_upper(j, h)

    for s in streams[len(weights):]:
        if s.parent is None:
            s.start(started)
    each(share, "start")
    got_sq[me] = sq[...]
    each(exchange, "wait_send")
    acc_q[...] = jnp.zeros_like(acc_q)
    acc_kv[...] = jnp.zeros_like(acc_kv)
    left = {}
    for s in streams:
        kind = s.group[0] if s.group[0] == "weight" else s.group[1]
        left[kind] = left.get(kind, 0) + 1
    scaled = []

    def scale_rows():
        each(share, "wait_recv")
        mean = jnp.sum(got_sq[...], axis=0) * (1.0 / (N_SEQ * COLS))
        inverse = lax.rsqrt(mean + EPS)
        eye = iota((128, 128), 0) == iota((128, 128), 1)
        for half in range(2):
            line = jnp.broadcast_to(inverse[half:half + 1], (128, 128))
            column = jnp.sum(jnp.where(eye, line, 0.0), axis=1, keepdims=True)
            scale[pl.ds(128 * half, 128), :] = jnp.broadcast_to(column, (128, 128))

    def multiply(h, n):
        def body(i, carry):
            sign = 1 - 2 * (i // NY)
            d = ((z + sign * h + NZ) % NZ) * NY + i % NY
            gains = gain[0:1, pl.ds(pl.multiple_of(d * COLS, COLS), COLS)]
            wide = jnp.concatenate([scale[...], scale[...]], axis=1)
            normed = (rows[d].astype(F32) * wide * gains).astype(BF16)
            p, half = d // 2, d % 2
            q_at = pl.multiple_of(half * 256, 256)
            kv_at = pl.multiple_of(512 + half * 64, 64)
            acc_q[...] += mm(normed, wbuf[p, pl.ds(q_at, 256), :])
            acc_kv[...] += mm(wbuf[p, pl.ds(kv_at, 64), :], normed, ((1,), (1,)))
            return carry

        lax.fori_loop(0, n, body, 0)

    waiting = [0, 1, 2, 3, 4]

    def row_step(stream, time, later):
        kind = stream.group[0] if stream.group[0] == "weight" else stream.group[1]
        left[kind] -= 1
        if left["weight"]:
            return
        for h in list(waiting):
            if left[h] == 0:
                if not scaled:
                    scaled.append(scale_rows())
                multiply(h, 4 if h in (0, 4) else 8)
                waiting.remove(h)

    run(streams, started, row_step)
    assert not waiting

    def turn_query(head):
        one = acc_q[:, pl.ds(HEAD * head, HEAD)]
        turned = one * cosine[...] + pltpu.roll(one, HEAD // 2, 1) * sine[...]
        query[head] = turned.astype(BF16)

    kv[...] = acc_kv[...].astype(BF16)
    turn_query(0)
    quad = [
        rdma(kv, parts.at[y], quad_send.at[k], quad_recv.at[k], {"seq": z * NY + (y + k) % NY})
        for k in range(1, NY)
    ]
    for copy in quad:
        copy.start()
    parts[y] = kv[...]
    turn_query(1)
    for copy in quad:
        copy.wait()
    both = jnp.concatenate([parts[i, pl.ds(0, 32), :] for i in range(NY)], axis=0).astype(F32)
    low, high = both[:64], both[64:]
    cos, sin = cos_t[...], sin_t[...]
    keys[blk, pl.ds(0, 64), :] = (low * cos - high * sin).astype(BF16)
    keys[blk, pl.ds(64, 64), :] = (high * cos + low * sin).astype(BF16)
    for i in range(NY):
        keys[blk, pl.ds(128 + 32 * i, 32), :] = parts[i, pl.ds(32, 32), :]

    key_streams = plane_streams(keys, k_send, k_recv, 1.5, ((0, 128), (128, 128)), "key", 0.0)
    for s in key_streams:
        if s.parent is None:
            s.start(started)

    unit = float(HEAD) ** (-0.5)

    def attend(origin, diagonal):
        for head in range(2):
            s = mm(query[head], keys[origin, pl.ds(0, HEAD), :]) * unit
            if diagonal:
                s = jnp.where(iota((256, 256), 1) <= iota((256, 256), 0), s, -1e30)
            high = jnp.max(s, axis=1, keepdims=True)
            if diagonal:
                new = jnp.broadcast_to(high, (256, HEAD))
            else:
                old = top[head]
                new = jnp.maximum(old, high)
                fade = jnp.exp(old - new)
            w = jnp.exp(s - jnp.concatenate([new, new], axis=1))
            part = w[:, :HEAD] + w[:, HEAD:]
            mix = mm(w.astype(BF16), keys[origin, pl.ds(HEAD, HEAD), :], ((1,), (1,)))
            top[head] = new
            total[head] = part if diagonal else total[head] * fade + part
            acc[head] = mix if diagonal else acc[head] * fade + mix

    attend(blk, True)
    seen, ready = {}, []
    clock = [1.0]

    def attend_earlier(name):
        kind, dx, other = LANDS[name]
        origin = blk_of(yl if kind == 0 else 1 - yl, x + dx, 1 - core if other else core)

        @pl.when(origin < blk)
        def _():
            attend(origin, False)

    def key_step(stream, time, later):
        name = stream.group[1]
        seen[name] = seen.get(name, 0) + 1
        if seen[name] == 2:
            ready.append(name)
        clock[0] = max(clock[0], time)
        while ready and (later is None or clock[0] + 0.6 <= later):
            attend_earlier(ready.pop(0))
            clock[0] += 0.6

    run(key_streams, started, key_step)
    for name in ready:
        attend_earlier(name)
    for head in range(2):
        norm = jnp.sum(total[head], axis=1, keepdims=True)
        out[:, pl.ds(HEAD * head, HEAD)] = (acc[head] / norm).astype(BF16)
    for copy in started:
        copy.wait_send()
    each(share, "wait_send")


def on_device(tokens, seg_local, shard_counts, norm_gain, query_weight, keyval_weight):
    rows_in_group = N_SEQ * 8
    vmem = pl.BlockSpec(memory_space=pltpu.VMEM)
    anywhere = pl.BlockSpec(memory_space=pltpu.HBM)
    dma = pltpu.SemaphoreType.DMA
    blk = lax.axis_index("blk")
    positions = (blk * rows_in_group + jnp.arange(rows_in_group, dtype=jnp.int32)).astype(F32)
    half = HEAD // 2
    frequency = THETA ** (-(jnp.arange(half, dtype=F32) * 2.0 / HEAD))
    angles = positions[:, None] * frequency[None, :]
    cos, sin = jnp.cos(angles), jnp.sin(angles)
    cos2 = jnp.concatenate([cos, cos], axis=1)
    sin2 = jnp.concatenate([-sin, sin], axis=1)
    kv_t = keyval_weight.reshape(512, 64).T
    return pl.pallas_call(
        layer_kernel,
        out_shape=jax.ShapeDtypeStruct((256, 256), BF16),
        in_specs=[anywhere, vmem, vmem, anywhere, anywhere] + [vmem] * 5,
        out_specs=vmem,
        scratch_shapes=[
            pltpu.VMEM((128, N_SEQ * COLS), BF16),
            pltpu.VMEM((N_SEQ, SLOTS, COLS), BF16),
            pltpu.VMEM((N_SEQ, 8, 128), F32),
            pltpu.VMEM((N_SEQ, SLOTS, COLS), BF16),
            pltpu.VMEM((N_SEQ + 1, 8, 128), F32),
            pltpu.VMEM((2, 128), F32),
            pltpu.VMEM((N_SEQ, 2, 128), F32),
            pltpu.VMEM((N_SEQ, 256, COLS), BF16),
            pltpu.VMEM((N_BLK, 640, 256), BF16),
            pltpu.VMEM((256, 128), F32),
            pltpu.VMEM((256, 256), F32),
            pltpu.VMEM((64, 256), F32),
            pltpu.VMEM((2, 256, HEAD), BF16),
            pltpu.VMEM((64, 256), BF16),
            pltpu.VMEM((NY, 64, 256), BF16),
            pltpu.VMEM((N_BLK, 256, 256), BF16),
            pltpu.VMEM((2, 256, HEAD), F32),
            pltpu.VMEM((2, 256, HEAD), F32),
            pltpu.VMEM((2, 256, HEAD), F32),
            dma((4,)), dma((3,)),
            dma((2, N_SEQ)), dma((2, N_SEQ)),
            dma((N_SEQ,)), dma((N_SEQ,)),
            dma((62,)), dma((62,)),
            dma((15,)), dma((15,)),
            dma((NY,)), dma((NY,)),
            dma((30,)), dma((30,)),
        ],
        compiler_params=pltpu.CompilerParams(
            collective_id=0, has_side_effects=True, vmem_limit_bytes=48 << 20),
        name="layer",
    )(tokens, seg_local.reshape(1, 128), jnp.broadcast_to(shard_counts, (1, 128)), query_weight,
      kv_t, norm_gain.reshape(1, N_SEQ * COLS), cos2, sin2, cos.T, sin.T)


def solution(mesh):
    return jax.shard_map(
        on_device,
        mesh=mesh,
        in_specs=(
            P(("blk", "seq"), None),
            P(("blk", "seq")),
            P("blk", "seq"),
            P(),
            P("blk", "seq"),
            P("blk", None, "seq"),
        ),
        out_specs=P("blk", "seq"),
        check_vma=False,
    )
```

time: 524 us -> 110 us (0.21)
  waiting for transfers between devices: 421 us -> 0 us
  Pallas kernels: 0 us -> 103 us
  blocking collectives: 26.5 us -> 0 us
  matrix products: 22.8 us -> 0 us
  between operations: 18.2 us -> 0.71 us
  other arithmetic: 15.1 us -> 0.99 us
  starting transfers between devices: 10.2 us -> 0 us
    psum x1 -> x0, waiting for transfers between devices: 331 us -> none  [on_device(): group_rows = lax.psum(placed.astype(jnp.bfloat16), 'seq')]
    pallas_call x0 -> x1, Pallas kernels: none -> 103 us  [on_device(): pl.pallas_call(layer_kernel, out_shape=jax.ShapeDtypeStruct((256, 256), B...]
    all_gather x4 -> x0, waiting for transfers between devices: 77.4 us -> none  [the longest x1 44.9 us: on_device(): key_rows = lax.all_gather(own_keys, 'blk', axis=0, tiled=True)]
    squeeze x1 -> x0, blocking collectives: 26.5 us -> none  [on_device(): counts_all = lax.all_gather(shard_counts, 'seq', axis=1, tiled=True)[0]]
    dot_general x6 -> x0, matrix products: 22.8 us -> none  [the longest x1 5.64 us: on_device(): jnp.einsum('qhk,kd->qhd', weights.astype(jnp.bfloat16), value_rows, prefe...]
    ppermute x4 -> x0, waiting for transfers between devices: 11.7 us -> none  [the longest x2 11.7 us: from_partner(): return lax.ppermute(value, axis, pairs)]
    ppermute x4 -> x0, starting transfers between devices: 9.86 us -> none  [the longest x2 6.02 us: from_behind(): return lax.ppermute(block, axis, route)]
    reduce_sum x4 -> x0, other arithmetic: 6.98 us -> none  [the longest x1 3.1 us: on_device(): jnp.mean(widened * widened, axis=-1, keepdims=True) + norm_eps]
  transfers between devices with their start and end apart: 9 -> 0, of which waited for: 5 -> 0; matrix products, arithmetic and copies ran while one was open for 6% -> 0% of each run, Pallas kernels for 0% -> 0%
where the time goes in v2:
time: 110 us
  Pallas kernels  103 us (94%)
  local copies, waits for them, and re-layouts  5.45 us (5%)
    pallas_call x1, Pallas kernels, on_device(): pl.pallas_call(layer_kernel, out_shape=jax.ShapeDtypeStruct((256, 256), B...  103 us
    unnamed x11, local copies, waits for them, and re-layouts  5.44 us

profile of v2, /device:TPU:1, one launch (start us, length us, event | category | flops | bytes accessed | tf_op | source)
XLA Modules:
  0.0 109.8 jit_solution(17092561334868259327)
XLA Ops:
  0.0 0.5 fusion
  0.6 0.1 pad_maximum_fusion
  0.7 0.3 multiply_sine_fusion.1
  1.7 0.0 copy-start
  1.7 1.6 %copy-done = bf16[128,8192]{1,0:T(8,128)(2,1)S(1)} copy-done((bf16[128,8192]{1,0:T(8,128)(2,1)S(1)}, bf16[128,8192]{1,0:T(8,128)(2,1)}, u32[]{:S(2)}) %copy-start) | copy-done | bytes 2097176
  3.3 0.0 copy-start.1
  3.3 0.9 copy-done.1
  4.2 0.0 copy-start.2
  4.2 0.8 copy-done.2
  5.1 0.0 copy-start.3
  5.1 0.8 copy-done.3
  5.8 0.0 copy-start.4
  5.8 0.7 copy-done.4
  6.5 102.7 %layer.1 = bf16[256,256]{1,0:T(8,128)(2,1)S(1)} custom-call(bf16[128,8192]{1,0:T(8,128)(2,1)S(1)} %copy-done, s32[1,128]{1,0:T(1,128)S(1)} %bitcast.9, s32[1,128]{1,0:T(1,128)S(1)} %broadcast_in_dim.10.count, bf16[512,256]{1,0:T(8,128)(2,1)S(1)} %copy-done.1, bf16[64,512]{1,0:T(8,128)(2,1)S(1)} %bitcast.7, f32[1,8192]{1,0:T(1,128)S(1)} %bitcast.8, ...), custom_call_target="tpu_custom_call" | custom-call | tf_op jit(solution)/shard_map/layer/pallas_call | solution.py:482
  109.1 0.7 copy.9
  (3 shorter events, 0.0 us)
Async XLA Ops:
  1.7 1.6 %copy-start = (bf16[128,8192]{1,0:T(8,128)(2,1)S(1)}, bf16[128,8192]{1,0:T(8,128)(2,1)}, u32[]{:S(2)}) copy-start(bf16[128,8192]{1,0:T(8,128)(2,1)} %tokens.1) | copy-start | bytes 6291460
  3.3 0.9 copy-start.1
  4.2 0.8 copy-start.2
  5.1 0.8 copy-start.3
  5.8 0.7 copy-start.4

commit v3 on v2

--- a/solution.py
+++ b/solution.py
@@ -14,7 +14,7 @@
 NX, NYL, NC = 4, 2, 2
 N_SEQ = NZ * NY
 N_BLK = NYL * NX * NC
-UPPER = 176
+UPPER = 192
 THETA = 500000.0
 EPS = 1e-05
 F32 = jnp.float32
@@ -38,7 +38,7 @@
         self.make().wait_recv()
 
 
-def schedule(streams):
+def schedule(streams, margin):
     by_name = {s.name: i for i, s in enumerate(streams)}
     children = {i: [] for i in range(len(streams))}
     heap, actions = [], []
@@ -56,15 +56,18 @@
             actions.append((ready, 0, i))
         end = max(ready, free.get(s.link, 0.0)) + s.cost
         free[s.link] = end
-        actions.append((end + s.lag, 1, i))
+        actions.append((end + s.lag + (0.0 if children[i] else margin), 1, i))
         for c in children[i]:
             heapq.heappush(heap, (end + s.lag, c))
     return sorted(actions), children
 
 
-def run(streams, started, after):
-    actions, children = schedule(streams)
-    for k, (time, kind, i) in enumerate(actions):
+def drive(streams, plan, first, limit, started, after):
+    actions, children = plan
+    for k in range(first, len(actions)):
+        time, kind, i = actions[k]
+        if limit is not None and time > limit:
+            return k
         if kind == 0:
             if not streams[i].begun:
                 streams[i].start(started)
@@ -74,6 +77,7 @@
             streams[c].start(started)
         later = [t for t, kd, j in actions[k + 1:] if kd == 0 or children[j]]
         after(streams[i], time, later[0] if later else None)
+    return len(actions)
 
 
 def rdma(src, dst, send, recv, where):
@@ -151,10 +155,10 @@
 
 
 def layer_kernel(
-    tokens, seg, count, q_weight, kv_weight, gain, cosine, sine, cos_t, sin_t, out,
-    tok, main, extra, got_main, got_extra, sq, got_sq, rows, wbuf, scale, acc_q, acc_kv,
+    tokens, seg_hbm, count_hbm, q_weight, kv_weight, gain_hbm, freq_hbm, out,
+    seg, count, gain, freq, cosine, sine, cos_t, sin_t, tok, main, extra, got_main, got_extra, sq, got_sq, rows, wbuf, scale, acc_q, acc_kv,
     query, kv, parts, keys, top, total, acc,
-    tok_sem, own_sem, a2a_send, a2a_recv, sq_send, sq_recv, r_send, r_recv,
+    small_sem, tok_sem, own_sem, a2a_send, a2a_recv, sq_send, sq_recv, r_send, r_recv,
     w_send, w_recv, quad_send, quad_recv, k_send, k_recv,
 ):
     me = lax.axis_index("seq")
@@ -185,12 +189,19 @@
         pltpu.make_async_copy(kv_weight.at[:, pl.ds(256, 256)], wbuf.at[blk, pl.ds(576, 64)],
                               own_sem.at[2]),
     ]
-    for load in token_loads + own_loads:
+    smalls = [
+        pltpu.make_async_copy(src, dst, small_sem.at[i])
+        for i, (src, dst) in enumerate((
+            (seg_hbm, seg), (count_hbm, count), (gain_hbm, gain), (freq_hbm, freq)))
+    ]
+    for load in smalls[:2] + token_loads + own_loads + smalls[2:]:
         load.start()
     lax.fori_loop(1, N_SEQ, greet, 0)
     for peer in plane_peers():
         pl.semaphore_signal(barrier, inc=1, device_id={"blk": peer}, device_id_type=MESH)
 
+    for load in smalls[:2]:
+        load.wait()
     slot = iota((SLOTS, 128), 0)
     member = (seg[...] == slot).astype(F32)
     sizes = jnp.sum(member, axis=1, keepdims=True)
@@ -199,24 +210,20 @@
     tail_pick = is_tail[:, 0:1]
     tail_size = jnp.sum(sizes * is_tail, axis=0, keepdims=True)
     safe = jnp.maximum(sizes, 1.0)
-    count_row = count[...].astype(F32)
-    lead_size = jnp.broadcast_to(sizes[0:1], (1, 128))
-
-    def pool(d, carry):
-        column = pl.multiple_of(d * COLS, COLS)
-        sums = mm(member, tok[:, pl.ds(column, COLS)])
-        main[d] = (sums / safe).astype(BF16)
-        tail = jnp.sum(sums * tail_pick, axis=0, keepdims=True)
-        extra[d] = jnp.concatenate(
-            [sums[0:1, :128], sums[0:1, 128:], tail[:, :128], tail[:, 128:],
-             count_row, lead_size, tail_size, jnp.zeros((1, 128), F32)], axis=0)
-        return carry
+    meta = jnp.concatenate(
+        [count[...].astype(F32), jnp.broadcast_to(sizes[0:1], (1, 64)), tail_size[:, :64]], axis=1)
+    top_row = iota((SLOTS, COLS), 0) == 0
 
     for i in range(4):
         token_loads[i].wait()
-        lax.fori_loop(8 * i, 8 * i + 8, pool, 0)
-    got_extra[0] = jnp.zeros((8, 128), F32)
-    for load in own_loads:
+        for d in range(8 * i, 8 * i + 8):
+            sums = mm(member, tok[:, pl.ds(d * COLS, COLS)])
+            main[d] = jnp.where(top_row, meta, sums / safe).astype(BF16)
+            tail = jnp.sum(sums * tail_pick, axis=0, keepdims=True)
+            extra[d] = jnp.concatenate(
+                [sums[0:1, :128], sums[0:1, 128:], tail[:, :128], tail[:, 128:]], axis=0)
+    got_extra[0] = jnp.zeros((4, 128), F32)
+    for load in own_loads + smalls[2:]:
         load.wait()
     pl.semaphore_wait(barrier, N_SEQ - 1 + 4)
 
@@ -240,28 +247,136 @@
         lax.fori_loop(1, N_SEQ, body, 0)
 
     started = []
-    weights = plane_streams(wbuf, w_send, w_recv, 7.3, ((0, 640),), "weight", 12.0)
+    weights = plane_streams(wbuf, w_send, w_recv, 1.9, [(160 * i, 160) for i in range(4)],
+                            "weight", 0.0)
+    streams = list(weights)
+    counter = [0]
+
+    def add(name, link, cost, lag, parent, part, origin, target, group):
+        sem = counter[0]
+        counter[0] += 1
+        at, size = ((0, UPPER), (UPPER, 256 - UPPER))[part]
+        piece = rows.at[seq_of(z + origin[0], y + origin[1]), pl.ds(at, size)]
+        where = {"seq": seq_of(z + target[0], y + target[1])}
+
+        def make():
+            return rdma(piece, piece, r_send.at[sem], r_recv.at[sem], where)
+
+        streams.append(Stream(name, link, cost, lag, parent, make, ("row", group),
+                              13.0 if parent is None else 0.0))
+
+    zc = (0.01138 * UPPER, 0.01138 * (256 - UPPER))
+    yc = (0.0125 * UPPER, 0.0125 * (256 - UPPER))
+    dys = (0, -turn, turn, 2)
+    hops = ((4, 3), (3, 4), (4, 3), (3, 4))
+    own = ("yA", "yB", "yC")
+
+    def z_upper(j, h):
+        for side, step in ((0, 1), (1, -1)):
+            if h < hops[j][side]:
+                parent = ("z", j, side, h - 1) if h else (None if j == 0 else own[j - 1])
+                add(("z", j, side, h), "z%d" % side, zc[0], 1.7, parent, 0,
+                    (-step * h, dys[j]), (step, 0), h + 1)
+
+    def y_all(tag, parent, part, dz, group):
+        names = own if tag is None else tuple((n, tag) for n in own)
+        add(names[0], "y", yc[part], 2.4, parent, part, (dz, 0), (0, turn), group)
+        add(names[1], "y", yc[part], 2.4, parent, part, (dz, 0), (0, -turn), group)
+        add(names[2], "y", yc[part], 2.4, names[0], part, (dz, -turn), (0, turn), group)
+
+    z_upper(0, 0)
+    y_all(None, None, 0, 0, 0)
+    for side, step in ((0, turn), (1, -turn)):
+        for h in range((4, 3)[side]):
+            add(("zz", side, h), "z%d" % side, zc[1], 1.7, ("zz", side, h - 1) if h else None, 1,
+                (-step * h, 0), (step, 0), h + 1)
+            y_all(("zz", side, h), ("zz", side, h), 1, -step * (h + 1), h + 1)
+    y_all("zz", None, 1, 0, 0)
+    for h in range(4):
+        for j in range(4):
+            if (j, h) != (0, 0):
+                z_upper(j, h)
+
+    left = {}
+    for s in streams:
+        kind = s.group[0] if s.group[0] == "weight" else s.group[1]
+        left[kind] = left.get(kind, 0) + 1
+    scaled = []
+
+    def scale_rows():
+        each(share, "wait_recv")
+        mean = jnp.sum(got_sq[...], axis=0) * (1.0 / (N_SEQ * COLS))
+        inverse = lax.rsqrt(mean + EPS)
+        eye = iota((128, 128), 0) == iota((128, 128), 1)
+        for half in range(2):
+            line = jnp.broadcast_to(inverse[half:half + 1], (128, 128))
+            column = jnp.sum(jnp.where(eye, line, 0.0), axis=1, keepdims=True)
+            scale[pl.ds(128 * half, 128), :] = jnp.broadcast_to(column, (128, 128))
+
+    def multiply(h, n):
+        def body(i, carry):
+            sign = 1 - 2 * (i // NY)
+            d = ((z + sign * h + NZ) % NZ) * NY + i % NY
+            gains = gain[0:1, pl.ds(pl.multiple_of(d * COLS, COLS), COLS)]
+            wide = jnp.concatenate([scale[...], scale[...]], axis=1)
+            normed = (rows[d].astype(F32) * wide * gains).astype(BF16)
+            p, half = d // 2, d % 2
+            q_at = pl.multiple_of(half * 256, 256)
+            kv_at = pl.multiple_of(512 + half * 64, 64)
+            acc_q[...] += mm(normed, wbuf[p, pl.ds(q_at, 256), :])
+            acc_kv[...] += mm(wbuf[p, pl.ds(kv_at, 64), :], normed, ((1,), (1,)))
+            return carry
+
+        lax.fori_loop(0, n, body, 0)
+
+    waiting = [0, 1, 2, 3, 4]
+
+    def row_step(stream, time, later):
+        kind = stream.group[0] if stream.group[0] == "weight" else stream.group[1]
+        left[kind] -= 1
+        if left["weight"]:
+            return
+        for h in list(waiting):
+            if left[h] == 0:
+                if not scaled:
+                    scaled.append(scale_rows())
+                multiply(h, 4 if h in (0, 4) else 8)
+                waiting.remove(h)
+
+    plan = schedule(streams, 2.5)
     each(exchange, "start")
     for s in weights:
         if s.parent is None and s.delay == 0.0:
             s.start(started)
     got_main[me] = main[me]
     got_extra[me + 1] = extra[me]
+    spot = (blk * 256 + iota((256, HEAD), 0)).astype(F32)
+    angle = spot * freq[...]
+    cosine[...] = jnp.cos(angle)
+    sine[...] = jnp.sin(angle)
+    cos_t[...] = cosine[...].T[:64]
+    sin_t[...] = sine[...].T[:64]
+    sine[...] = jnp.where(iota((256, HEAD), 1) < HEAD // 2, -sine[...], sine[...])
+    at = drive(streams, plan, 0, 9.5, started, row_step)
     each(exchange, "wait_recv")
 
     slots_all = N_SEQ * SLOTS
-    counts16 = got_extra[1:N_SEQ + 1, 4, :].astype(BF16)
+    slots = got_main[...].reshape(slots_all, COLS)
+    heads = (iota((N_SEQ, slots_all), 1) == SLOTS * iota((N_SEQ, slots_all), 0)).astype(BF16)
+    metas = mm(heads, slots)
+    counts16 = metas[:, :128].astype(BF16)
     source = iota((N_SEQ, slots_all), 0)
     owner = iota((N_SEQ, slots_all), 1) // SLOTS
     before = mm(counts16, (source < owner).astype(BF16), ((0,), (0,)))
     inside = mm(counts16, (source == owner).astype(BF16), ((0,), (0,)))
     rank = (iota((128, slots_all), 1) % SLOTS).astype(F32)
-    lead_sizes = got_extra[1:N_SEQ + 1, 5, :] + got_extra[0:N_SEQ, 6, :]
+    tails = metas[:, 192:193]
+    tails = jnp.concatenate([jnp.zeros((1, 1), F32), tails[:N_SEQ - 1]], axis=0)
+    lead_sizes = metas[:, 128:129] + tails
     border = jnp.concatenate(
         [(got_extra[1:N_SEQ + 1, i, :] + got_extra[0:N_SEQ, 2 + i, :]) / lead_sizes
          for i in range(2)], axis=1).astype(BF16)
     spread = (iota((slots_all, N_SEQ), 0) // SLOTS == iota((slots_all, N_SEQ), 1)).astype(BF16)
-    slots = got_main[...].reshape(slots_all, COLS)
     first = iota((slots_all, COLS), 0) % SLOTS == 0
     slots = jnp.where(first, mm(spread, border), slots.astype(F32)).astype(BF16)
     ones = jnp.ones((8, COLS), BF16)
@@ -277,53 +392,6 @@
         across = mm(ones, coarse, ((1,), (1,))) + mm(ones, fine, ((1,), (1,)))
         sq[half:half + 1, :] = across[0:1]
 
-    streams = list(weights)
-    counter = [0]
-
-    def add(name, link, cost, lag, parent, part, origin, target, group):
-        sem = counter[0]
-        counter[0] += 1
-        at, size = ((0, UPPER), (UPPER, 256 - UPPER))[part]
-        piece = rows.at[seq_of(z + origin[0], y + origin[1]), pl.ds(at, size)]
-        where = {"seq": seq_of(z + target[0], y + target[1])}
-
-        def make():
-            return rdma(piece, piece, r_send.at[sem], r_recv.at[sem], where)
-
-        streams.append(Stream(name, link, cost, lag, parent, make, ("row", group),
-                              13.0 if parent is None else 0.0))
-
-    zc, yc = (2.0, 0.95), (2.0, 0.95)
-    dys = (0, -turn, turn, 2)
-    hops = ((4, 3), (3, 4), (4, 3), (3, 4))
-    own = ("yA", "yB", "yC")
-
-    def z_upper(j, h):
-        for side, step in ((0, 1), (1, -1)):
-            if h < hops[j][side]:
-                parent = ("z", j, side, h - 1) if h else (None if j == 0 else own[j - 1])
-                add(("z", j, side, h), "z%d" % side, zc[0], 1.7, parent, 0,
-                    (-step * h, dys[j]), (step, 0), h + 1)
-
-    def y_all(tag, parent, part, dz, group):
-        names = own if tag is None else tuple((n, tag) for n in own)
-        add(names[0], "y", yc[part], 2.4, parent, part, (dz, 0), (0, turn), group)
-        add(names[1], "y", yc[part], 2.4, parent, part, (dz, 0), (0, -turn), group)
-        add(names[2], "y", yc[part], 2.4, names[0], part, (dz, -turn), (0, turn), group)
-
-    z_upper(0, 0)
-    y_all(None, None, 0, 0, 0)
-    for side, step in ((0, turn), (1, -turn)):
-        for h in range((4, 3)[side]):
-            add(("zz", side, h), "z%d" % side, zc[1], 1.7, ("zz", side, h - 1) if h else None, 1,
-                (-step * h, 0), (step, 0), h + 1)
-            y_all(("zz", side, h), ("zz", side, h), 1, -step * (h + 1), h + 1)
-    y_all("zz", None, 1, 0, 0)
-    for h in range(4):
-        for j in range(4):
-            if (j, h) != (0, 0):
-                z_upper(j, h)
-
     for s in streams[len(weights):]:
         if s.parent is None:
             s.start(started)
@@ -332,53 +400,7 @@
     each(exchange, "wait_send")
     acc_q[...] = jnp.zeros_like(acc_q)
     acc_kv[...] = jnp.zeros_like(acc_kv)
-    left = {}
-    for s in streams:
-        kind = s.group[0] if s.group[0] == "weight" else s.group[1]
-        left[kind] = left.get(kind, 0) + 1
-    scaled = []
-
-    def scale_rows():
-        each(share, "wait_recv")
-        mean = jnp.sum(got_sq[...], axis=0) * (1.0 / (N_SEQ * COLS))
-        inverse = lax.rsqrt(mean + EPS)
-        eye = iota((128, 128), 0) == iota((128, 128), 1)
-        for half in range(2):
-            line = jnp.broadcast_to(inverse[half:half + 1], (128, 128))
-            column = jnp.sum(jnp.where(eye, line, 0.0), axis=1, keepdims=True)
-            scale[pl.ds(128 * half, 128), :] = jnp.broadcast_to(column, (128, 128))
-
-    def multiply(h, n):
-        def body(i, carry):
-            sign = 1 - 2 * (i // NY)
-            d = ((z + sign * h + NZ) % NZ) * NY + i % NY
-            gains = gain[0:1, pl.ds(pl.multiple_of(d * COLS, COLS), COLS)]
-            wide = jnp.concatenate([scale[...], scale[...]], axis=1)
-            normed = (rows[d].astype(F32) * wide * gains).astype(BF16)
-            p, half = d // 2, d % 2
-            q_at = pl.multiple_of(half * 256, 256)
-            kv_at = pl.multiple_of(512 + half * 64, 64)
-            acc_q[...] += mm(normed, wbuf[p, pl.ds(q_at, 256), :])
-            acc_kv[...] += mm(wbuf[p, pl.ds(kv_at, 64), :], normed, ((1,), (1,)))
-            return carry
-
-        lax.fori_loop(0, n, body, 0)
-
-    waiting = [0, 1, 2, 3, 4]
-
-    def row_step(stream, time, later):
-        kind = stream.group[0] if stream.group[0] == "weight" else stream.group[1]
-        left[kind] -= 1
-        if left["weight"]:
-            return
-        for h in list(waiting):
-            if left[h] == 0:
-                if not scaled:
-                    scaled.append(scale_rows())
-                multiply(h, 4 if h in (0, 4) else 8)
-                waiting.remove(h)
-
-    run(streams, started, row_step)
+    drive(streams, plan, at, None, started, row_step)
     assert not waiting
 
     def turn_query(head):
@@ -406,7 +428,8 @@
     for i in range(NY):
         keys[blk, pl.ds(128 + 32 * i, 32), :] = parts[i, pl.ds(32, 32), :]
 
-    key_streams = plane_streams(keys, k_send, k_recv, 1.5, ((0, 128), (128, 128)), "key", 0.0)
+    key_streams = plane_streams(keys, k_send, k_recv, 0.75, [(64 * i, 64) for i in range(4)],
+                                "key", 0.0)
     for s in key_streams:
         if s.parent is None:
             s.start(started)
@@ -447,49 +470,50 @@
     def key_step(stream, time, later):
         name = stream.group[1]
         seen[name] = seen.get(name, 0) + 1
-        if seen[name] == 2:
+        if seen[name] == 4:
             ready.append(name)
         clock[0] = max(clock[0], time)
         while ready and (later is None or clock[0] + 0.6 <= later):
             attend_earlier(ready.pop(0))
             clock[0] += 0.6
 
-    run(key_streams, started, key_step)
+    drive(key_streams, schedule(key_streams, 0.0), 0, None, started, key_step)
     for name in ready:
         attend_earlier(name)
     for head in range(2):
         norm = jnp.sum(total[head], axis=1, keepdims=True)
-        out[:, pl.ds(HEAD * head, HEAD)] = (acc[head] / norm).astype(BF16)
+        out[:, pl.ds(HEAD * head, HEAD)] = acc[head] / norm
     for copy in started:
         copy.wait_send()
     each(share, "wait_send")
 
 
 def on_device(tokens, seg_local, shard_counts, norm_gain, query_weight, keyval_weight):
-    rows_in_group = N_SEQ * 8
     vmem = pl.BlockSpec(memory_space=pltpu.VMEM)
     anywhere = pl.BlockSpec(memory_space=pltpu.HBM)
     dma = pltpu.SemaphoreType.DMA
-    blk = lax.axis_index("blk")
-    positions = (blk * rows_in_group + jnp.arange(rows_in_group, dtype=jnp.int32)).astype(F32)
     half = HEAD // 2
-    frequency = THETA ** (-(jnp.arange(half, dtype=F32) * 2.0 / HEAD))
-    angles = positions[:, None] * frequency[None, :]
-    cos, sin = jnp.cos(angles), jnp.sin(angles)
-    cos2 = jnp.concatenate([cos, cos], axis=1)
-    sin2 = jnp.concatenate([-sin, sin], axis=1)
+    frequency = THETA ** (-((jnp.arange(HEAD, dtype=jnp.int32) % half).astype(F32) * 2.0 / HEAD))
     kv_t = keyval_weight.reshape(512, 64).T
-    return pl.pallas_call(
+    mixed = pl.pallas_call(
         layer_kernel,
-        out_shape=jax.ShapeDtypeStruct((256, 256), BF16),
-        in_specs=[anywhere, vmem, vmem, anywhere, anywhere] + [vmem] * 5,
+        out_shape=jax.ShapeDtypeStruct((256, 256), F32),
+        in_specs=[anywhere] * 7,
         out_specs=vmem,
         scratch_shapes=[
+            pltpu.VMEM((1, 128), jnp.int32),
+            pltpu.VMEM((1, 128), jnp.int32),
+            pltpu.VMEM((1, N_SEQ * COLS), F32),
+            pltpu.VMEM((1, HEAD), F32),
+            pltpu.VMEM((256, HEAD), F32),
+            pltpu.VMEM((256, HEAD), F32),
+            pltpu.VMEM((64, 256), F32),
+            pltpu.VMEM((64, 256), F32),
             pltpu.VMEM((128, N_SEQ * COLS), BF16),
             pltpu.VMEM((N_SEQ, SLOTS, COLS), BF16),
-            pltpu.VMEM((N_SEQ, 8, 128), F32),
+            pltpu.VMEM((N_SEQ, 4, 128), F32),
             pltpu.VMEM((N_SEQ, SLOTS, COLS), BF16),
-            pltpu.VMEM((N_SEQ + 1, 8, 128), F32),
+            pltpu.VMEM((N_SEQ + 1, 4, 128), F32),
             pltpu.VMEM((2, 128), F32),
             pltpu.VMEM((N_SEQ, 2, 128), F32),
             pltpu.VMEM((N_SEQ, 256, COLS), BF16),
@@ -504,19 +528,20 @@
             pltpu.VMEM((2, 256, HEAD), F32),
             pltpu.VMEM((2, 256, HEAD), F32),
             pltpu.VMEM((2, 256, HEAD), F32),
-            dma((4,)), dma((3,)),
+            dma((4,)), dma((4,)), dma((3,)),
             dma((2, N_SEQ)), dma((2, N_SEQ)),
             dma((N_SEQ,)), dma((N_SEQ,)),
             dma((62,)), dma((62,)),
-            dma((15,)), dma((15,)),
+            dma((60,)), dma((60,)),
             dma((NY,)), dma((NY,)),
-            dma((30,)), dma((30,)),
+            dma((60,)), dma((60,)),
         ],
         compiler_params=pltpu.CompilerParams(
-            collective_id=0, has_side_effects=True, vmem_limit_bytes=48 << 20),
+            collective_id=0, has_side_effects=True, vmem_limit_bytes=63 << 20),
         name="layer",
     )(tokens, seg_local.reshape(1, 128), jnp.broadcast_to(shard_counts, (1, 128)), query_weight,
-      kv_t, norm_gain.reshape(1, N_SEQ * COLS), cos2, sin2, cos.T, sin.T)
+      kv_t, norm_gain.reshape(1, N_SEQ * COLS), frequency.reshape(1, HEAD))
+    return mixed.astype(BF16)
 
 
 def solution(mesh):

time: 110 us -> 103 us (0.936)
  local copies, waits for them, and re-layouts: 5.45 us -> 0.57 us
  Pallas kernels: 103 us -> 99.1 us
  other arithmetic: 0.99 us -> 2.14 us
    unnamed x11 -> x0, local copies, waits for them, and re-layouts: 5.44 us -> none
    pallas_call x1, Pallas kernels: 103 us -> 99.1 us  [on_device(): pl.pallas_call(layer_kernel, out_shape=jax.ShapeDtypeStruct((256, 256), F...]
    convert_element_type x1, other arithmetic: 0.01 us -> 1.62 us  [on_device(): return mixed.astype(BF16)]
where the time goes in v3:
time: 103 us; the launch traced here: 102 us
  Pallas kernels  99.1 us (96%)
  other arithmetic  2.14 us (2%)
    pallas_call x1, Pallas kernels, on_device(): pl.pallas_call(layer_kernel, out_shape=jax.ShapeDtypeStruct((256, 256), F...  99.1 us

profile of v3, /device:TPU:1, one launch (start us, length us, event | category | flops | bytes accessed | tf_op | source)
XLA Modules:
  0.0 102.4 jit_solution(7719887576659777969)
XLA Ops:
  0.7 0.6 broadcast_in_dim.8.count_hbm
  1.2 0.5 fusion.3.freq_hbm
  1.7 99.1 %layer.1 = f32[256,256]{1,0:T(8,128)} custom-call(bf16[128,8192]{1,0:T(8,128)(2,1)} %tokens.1, s32[1,128]{1,0:T(1,128)} %bitcast.9, s32[1,128]{1,0:T(1,128)} %broadcast_in_dim.8.count_hbm, bf16[512,256]{1,0:T(8,128)(2,1)} %q_weight.1, bf16[64,512]{1,0:T(8,128)(2,1)} %bitcast.7, f32[1,8192]{1,0:T(1,128)} %bitcast.8, f32[1,128]{1,0:T(1,128)} %fusion.3.freq_hbm), custom_call_target="tpu_custom_call" | custom-call | tf_op jit(solution)/shard_map/layer/pallas_call | solution.py:498
  100.8 1.6 %convert_element_type.14 = bf16[256,256]{1,0:T(8,128)(2,1)} convert(f32[256,256]{1,0:T(8,128)} %layer.1) | non-fusion elementwise | flops 65536 | bytes 393216 | tf_op jit(solution)/shard_map/convert_element_type | solution.py:544

commit v4 on v3

--- a/solution.py
+++ b/solution.py
@@ -14,7 +14,7 @@
 NX, NYL, NC = 4, 2, 2
 N_SEQ = NZ * NY
 N_BLK = NYL * NX * NC
-UPPER = 192
+UPPER = 176
 THETA = 500000.0
 EPS = 1e-05
 F32 = jnp.float32
@@ -126,7 +126,7 @@
 }
 
 
-def plane_streams(buf, send, recv, cost, parts, group, pair_delay):
+def plane_streams(buf, send, recv, cost, parts, group):
     _, yl, x, c = blk_parts()
     targets = plane_peers()
     streams = []
@@ -142,7 +142,7 @@
             streams.append(Stream(
                 (name, p), link, cost / 5 if link == "core" else cost,
                 1.0 if link == "core" else 1.7, None if parent is None else (parent, p), make,
-                (group, name), pair_delay if name == "pair" else 0.0))
+                (group, name)))
     return streams
 
 
@@ -172,7 +172,8 @@
     barrier = pltpu.get_barrier_semaphore()
 
     def greet(k, carry):
-        pl.semaphore_signal(barrier, inc=1, device_id={"seq": (me + k) % N_SEQ},
+        far = (k + 13) % (N_SEQ - 1) + 1
+        pl.semaphore_signal(barrier, inc=1, device_id={"seq": (me + far) % N_SEQ},
                             device_id_type=MESH)
         return carry
 
@@ -240,7 +241,7 @@
 
     def each(copies, what):
         def body(k, carry):
-            for copy in copies(k):
+            for copy in copies((k + 13) % (N_SEQ - 1) + 1):
                 getattr(copy, what)()
             return carry
 
@@ -248,7 +249,7 @@
 
     started = []
     weights = plane_streams(wbuf, w_send, w_recv, 1.9, [(160 * i, 160) for i in range(4)],
-                            "weight", 0.0)
+                            "weight")
     streams = list(weights)
     counter = [0]
 
@@ -304,7 +305,9 @@
     scaled = []
 
     def scale_rows():
+        each(exchange, "wait_send")
         each(share, "wait_recv")
+        each(share, "wait_send")
         mean = jnp.sum(got_sq[...], axis=0) * (1.0 / (N_SEQ * COLS))
         inverse = lax.rsqrt(mean + EPS)
         eye = iota((128, 128), 0) == iota((128, 128), 1)
@@ -397,7 +400,6 @@
             s.start(started)
     each(share, "start")
     got_sq[me] = sq[...]
-    each(exchange, "wait_send")
     acc_q[...] = jnp.zeros_like(acc_q)
     acc_kv[...] = jnp.zeros_like(acc_kv)
     drive(streams, plan, at, None, started, row_step)
@@ -412,7 +414,7 @@
     turn_query(0)
     quad = [
         rdma(kv, parts.at[y], quad_send.at[k], quad_recv.at[k], {"seq": z * NY + (y + k) % NY})
-        for k in range(1, NY)
+        for k in (2, 1, 3)
     ]
     for copy in quad:
         copy.start()
@@ -429,10 +431,11 @@
         keys[blk, pl.ds(128 + 32 * i, 32), :] = parts[i, pl.ds(32, 32), :]
 
     key_streams = plane_streams(keys, k_send, k_recv, 0.75, [(64 * i, 64) for i in range(4)],
-                                "key", 0.0)
+                                "key")
+    key_started = []
     for s in key_streams:
         if s.parent is None:
-            s.start(started)
+            s.start(key_started)
 
     unit = float(HEAD) ** (-0.5)
 
@@ -456,6 +459,8 @@
             acc[head] = mix if diagonal else acc[head] * fade + mix
 
     attend(blk, True)
+    for copy in started:
+        copy.wait_send()
     seen, ready = {}, []
     clock = [1.0]
 
@@ -477,15 +482,14 @@
             attend_earlier(ready.pop(0))
             clock[0] += 0.6
 
-    drive(key_streams, schedule(key_streams, 0.0), 0, None, started, key_step)
+    drive(key_streams, schedule(key_streams, 0.0), 0, None, key_started, key_step)
     for name in ready:
         attend_earlier(name)
     for head in range(2):
         norm = jnp.sum(total[head], axis=1, keepdims=True)
         out[:, pl.ds(HEAD * head, HEAD)] = acc[head] / norm
-    for copy in started:
+    for copy in key_started:
         copy.wait_send()
-    each(share, "wait_send")
 
 
 def on_device(tokens, seg_local, shard_counts, norm_gain, query_weight, keyval_weight):

time: 103 us -> 100 us (0.971)
  Pallas kernels: 99.1 us -> 95.6 us
    pallas_call x1, Pallas kernels: 99.1 us -> 95.6 us  [on_device(): pl.pallas_call(layer_kernel, out_shape=jax.ShapeDtypeStruct((256, 256), F...]
where the time goes in v4:
time: 100 us; the launch traced here: 99 us
  Pallas kernels  95.6 us (96%)
  other arithmetic  2.14 us (2%)
    pallas_call x1, Pallas kernels, on_device(): pl.pallas_call(layer_kernel, out_shape=jax.ShapeDtypeStruct((256, 256), F...  95.6 us

profile of v4, /device:TPU:1, one launch (start us, length us, event | category | flops | bytes accessed | tf_op | source)
XLA Modules:
  0.0 99.0 jit_solution(12003397181023567428)
XLA Ops:
  0.7 0.6 broadcast_in_dim.8.count_hbm
  1.2 0.5 fusion.3.freq_hbm
  1.7 95.6 %layer.1 = f32[256,256]{1,0:T(8,128)} custom-call(bf16[128,8192]{1,0:T(8,128)(2,1)} %tokens.1, s32[1,128]{1,0:T(1,128)} %bitcast.9, s32[1,128]{1,0:T(1,128)} %broadcast_in_dim.8.count_hbm, bf16[512,256]{1,0:T(8,128)(2,1)} %q_weight.1, bf16[64,512]{1,0:T(8,128)(2,1)} %bitcast.7, f32[1,8192]{1,0:T(1,128)} %bitcast.8, f32[1,128]{1,0:T(1,128)} %fusion.3.freq_hbm), custom_call_target="tpu_custom_call" | custom-call | tf_op jit(solution)/shard_map/layer/pallas_call | solution.py:502
  97.3 1.6 %convert_element_type.14 = bf16[256,256]{1,0:T(8,128)(2,1)} convert(f32[256,256]{1,0:T(8,128)} %layer.1) | non-fusion elementwise | flops 65536 | bytes 393216 | tf_op jit(solution)/shard_map/convert_element_type | solution.py:548
